TPU v7x, 32 devices: a whole 2x2x4 slice. The times are simulated.
32 devices in a mesh: member: 4 (over z), region: 4 (over y, x), fine: 2 (over core).
Axes of the slice: x: 2, y: 2, z: 4, core: 2. Of those that a mesh axis runs over, the one named last changes fastest.
Arguments:
- sample_surface_elevation: float32 [256, 4, 512], P('member', 'region', 'fine'), may hold values from -6 to 6
- sample_zonal_current: float32 [256, 4, 512], P('member', 'region', 'fine'), may hold values from -6 to 6
- sample_meridional_current: float32 [256, 4, 512], P('member', 'region', 'fine'), may hold values from -6 to 6
- zonal_edge_layer_courant: float32 [4, 512], P('region', 'fine'), may hold values from 0.1 to 0.45
- meridional_edge_layer_courant: float32 [4, 512], P('region', 'fine'), may hold values from 0.1 to 0.45
- obs_index: int32 [64, 512, 4], P(('member', 'region', 'fine')), may hold values from 0 to 95
- obs_weight: float32 [64, 512, 4], P(('member', 'region', 'fine')), may hold values from 0.1 to 1
- obs_value: float32 [64, 512], P(('member', 'region', 'fine')), may hold values from -12 to 12
- obs_var: float32 [64, 512], P(('member', 'region', 'fine')), may hold values from 0.25 to 4
- obs_count: int32 [64], P(('member', 'region', 'fine')), may hold values from 64 to 512, as said below
- fine_ctrl: float32 [3, 8, 2, 512], P(None, 'region', 'fine', 'member'), may hold values from -6 to 6
Outputs:
- ana_h: float32 [256, 4, 512], P('member', 'region', 'fine')
- ana_u: float32 [256, 4, 512], P('member', 'region', 'fine')
- ana_v: float32 [256, 4, 512], P('member', 'region', 'fine')
- fine_out: float32 [3, 8, 2, 512], P(None, 'region', 'fine', 'member')
Inputs may be any that keep to these rules, and one draw needn't show every extreme that they name: `obs_count`: each region's count is 512 // 8 times 1, 2, 4 or 8; some region has 512 and some 512 // 8 in every draw; the live observations of a region are its first count slots.
All inputs are finite; a program needn't handle non-finite values.
Results may differ from a plain program's by a relative error of at most 0.0003.
Values sent between devices are 32-bit elements; how exact they have to be, the bound alone decides.
No kernel may reach another device: no remote copies, remote signals or barrier semaphores. Data moves between devices by JAX's collectives and lax.ppermute only.
A program may use at most 64 MiB of HBM per device.

v0:
```python
import jax
import jax.numpy as jnp
from jax import lax
from jax.sharding import PartitionSpec as P

REG_DEV = 2
STEPS = 4
NEWTON = 8


HIGHEST = lax.Precision.HIGHEST


def shifted(shard, axis, by):
    count = lax.axis_size(axis)
    pairs = [(i, i + by) for i in range(count) if 0 <= i + by < count]
    return lax.ppermute(shard, axis, pairs)


def passed_along(block, axis, distance):
    devices = range(lax.axis_size(axis))
    route = [((i - distance) % len(devices), i) for i in devices]
    return lax.ppermute(block, axis, route)


def analyse_regions(ensemble, obs_index, obs_weight, obs_value, obs_var, obs_count):
    members = ensemble.shape[0]
    obs_total = obs_value.shape[1]
    mean_state = jnp.mean(ensemble, axis=0)
    spread = ensemble - mean_state
    index_flat = obs_index.reshape(REG_DEV, -1)
    picked = jax.vmap(
        lambda column_block, positions: column_block[:, positions], in_axes=(1, 0), out_axes=1
    )(ensemble, index_flat)
    picked = picked.reshape(members, REG_DEV, obs_total, 4)
    predicted = jnp.sum(picked * obs_weight, axis=3)
    mean_obs = jnp.mean(predicted, axis=0)
    obs_spread = predicted - mean_obs
    active_obs = (jnp.arange(obs_total)[None, :] < obs_count[:, None]).astype(jnp.float32)
    weighted = obs_spread * (active_obs / obs_var)
    gram_sum = jnp.einsum("kro,jro->rkj", weighted, obs_spread, precision=HIGHEST)
    identity = jnp.eye(members, dtype=jnp.float32)
    scaled = identity + gram_sum / (members - 1)
    frobenius = jnp.sqrt(jnp.sum(scaled * scaled, axis=(1, 2)))
    iterate = scaled / frobenius[:, None, None]
    inverse_root = jnp.broadcast_to(identity, scaled.shape)
    for sweep in range(NEWTON):
        factor = 1.5 * identity - 0.5 * jnp.einsum(
            "rij,rjk->rik", inverse_root, iterate, precision=HIGHEST
        )
        iterate = jnp.einsum("rij,rjk->rik", iterate, factor, precision=HIGHEST)
        inverse_root = jnp.einsum("rij,rjk->rik", factor, inverse_root, precision=HIGHEST)
    transform = inverse_root / jnp.sqrt(frobenius)[:, None, None]
    innovation = jnp.einsum("kro,ro->rk", weighted, obs_value - mean_obs, precision=HIGHEST)
    halfway = jnp.einsum("rkj,rj->rk", transform, innovation, precision=HIGHEST)
    mean_weights = jnp.einsum("rkj,rj->rk", transform, halfway, precision=HIGHEST) / (members - 1)
    increment = jnp.einsum("rk,krs->rs", mean_weights, spread, precision=HIGHEST)
    analysis = (mean_state + increment)[None] + jnp.einsum(
        "rjk,jrs->krs", transform, spread, precision=HIGHEST
    )
    return (analysis, increment)


def shards(
    sample_surface_elevation,
    sample_zonal_current,
    sample_meridional_current,
    zonal_edge_layer_courant,
    meridional_edge_layer_courant,
    obs_index,
    obs_weight,
    obs_value,
    obs_var,
    obs_count,
    fine_ctrl,
):
    for pass_no in range(STEPS):
        flux_u = zonal_edge_layer_courant * sample_zonal_current
        flux_v = meridional_edge_layer_courant * sample_meridional_current
        below_row = shifted(flux_v, "region", 1)
        south_flux = jnp.concatenate([below_row, flux_v[:, :-1]], axis=1)
        west_column = passed_along(flux_u[:, :, -1:], "fine", 1)
        west_flux = jnp.concatenate([west_column, flux_u[:, :, :-1]], axis=2)
        sample_surface_elevation = sample_surface_elevation - (
            flux_u - west_flux + flux_v - south_flux
        )
        above_row = shifted(sample_surface_elevation, "region", -1)
        north_rows = jnp.concatenate([sample_surface_elevation[:, 1:], above_row], axis=1)
        east_column = passed_along(sample_surface_elevation[:, :, :1], "fine", -1)
        east_heights = jnp.concatenate([sample_surface_elevation[:, :, 1:], east_column], axis=2)
        sample_zonal_current = sample_zonal_current - (east_heights - sample_surface_elevation)
        sample_meridional_current = sample_meridional_current - (
            north_rows - sample_surface_elevation
        )
    member_groups = lax.axis_size("member")
    strip_groups = lax.axis_size("region")
    mem_local, rows_local, columns = sample_surface_elevation.shape
    region_cols = columns // (member_groups * strip_groups)
    members = mem_local * member_groups
    view_h = sample_surface_elevation.reshape(
        mem_local, rows_local, member_groups, strip_groups, region_cols
    )
    view_u = sample_zonal_current.reshape(
        mem_local, rows_local, member_groups, strip_groups, region_cols
    )
    view_v = sample_meridional_current.reshape(
        mem_local, rows_local, member_groups, strip_groups, region_cols
    )
    arrived = (
        lax.all_to_all(
            lax.all_to_all(view_h, "member", split_axis=2, concat_axis=0, tiled=True),
            "region",
            split_axis=3,
            concat_axis=1,
            tiled=True,
        ),
        lax.all_to_all(
            lax.all_to_all(view_u, "member", split_axis=2, concat_axis=0, tiled=True),
            "region",
            split_axis=3,
            concat_axis=1,
            tiled=True,
        ),
        lax.all_to_all(
            lax.all_to_all(view_v, "member", split_axis=2, concat_axis=0, tiled=True),
            "region",
            split_axis=3,
            concat_axis=1,
            tiled=True,
        ),
    )
    ensemble = jnp.concatenate([piece.reshape(members, REG_DEV, -1) for piece in arrived], axis=2)
    cells = ensemble.shape[2] // 3
    analysis, increment = analyse_regions(
        ensemble, obs_index, obs_weight, obs_value, obs_var, obs_count
    )
    split_vars = analysis.reshape(members, REG_DEV, 3, cells)
    back_h = split_vars[:, :, 0, :].reshape(members, strip_groups * rows_local, 1, 1, region_cols)
    back_u = split_vars[:, :, 1, :].reshape(members, strip_groups * rows_local, 1, 1, region_cols)
    back_v = split_vars[:, :, 2, :].reshape(members, strip_groups * rows_local, 1, 1, region_cols)
    home = (
        lax.all_to_all(
            lax.all_to_all(back_h, "member", split_axis=0, concat_axis=2, tiled=True),
            "region",
            split_axis=1,
            concat_axis=3,
            tiled=True,
        ),
        lax.all_to_all(
            lax.all_to_all(back_u, "member", split_axis=0, concat_axis=2, tiled=True),
            "region",
            split_axis=1,
            concat_axis=3,
            tiled=True,
        ),
        lax.all_to_all(
            lax.all_to_all(back_v, "member", split_axis=0, concat_axis=2, tiled=True),
            "region",
            split_axis=1,
            concat_axis=3,
            tiled=True,
        ),
    )
    ana_h = home[0].reshape(mem_local, rows_local, columns)
    ana_u = home[1].reshape(mem_local, rows_local, columns)
    ana_v = home[2].reshape(mem_local, rows_local, columns)
    by_variable = increment.reshape(REG_DEV, 3, cells).transpose(1, 0, 2)
    by_variable = by_variable.reshape(3, strip_groups * rows_local, region_cols)
    coarse_block = lax.all_to_all(by_variable, "region", split_axis=1, concat_axis=2, tiled=True)
    widened = jnp.repeat(jnp.repeat(coarse_block, 2, axis=1), 2, axis=2)
    fine_out = fine_ctrl + widened.reshape(fine_ctrl.shape)
    return (ana_h, ana_u, ana_v, fine_out)


def solution(mesh):
    return jax.shard_map(
        shards,
        mesh=mesh,
        in_specs=(
            P("member", "region", "fine"),
            P("member", "region", "fine"),
            P("member", "region", "fine"),
            P("region", "fine"),
            P("region", "fine"),
            P(("member", "region", "fine"), None, None),
            P(("member", "region", "fine"), None, None),
            P(("member", "region", "fine"), None),
            P(("member", "region", "fine"), None),
            P(("member", "region", "fine")),
            P(None, "region", "fine", "member"),
        ),
        out_specs=(
            P("member", "region", "fine"),
            P("member", "region", "fine"),
            P("member", "region", "fine"),
            P(None, "region", "fine", "member"),
        ),
        check_vma=False,
    )
```

profile of v0, /device:TPU:0, one launch (start us, length us, event | category | flops | bytes accessed | tf_op | source)
XLA Modules:
  0.0 257.8 jit_solution(5909376460938994211)
XLA Ops:
  2.4 4.9 %collective-permute-start.1 = (f32[64,1,256]{0,2,1:T(8,128)S(1)}, f32[64,1,256]{0,2,1:T(8,128)S(1)}, u32[]{:S(2)}, u32[]{:S(2)}) collective-permute-start(f32[64,1,256]{0,2,1:T(8,128)S(1)} %broadcast_multiply_fusion.3), channel_id=1, source_target_pairs={{0,2},{2,4},{4,6},{1,3},{3,5},{5,7},{8,10},{10,12},{12,14},{9,11},... | collective-permute-start | bytes 196616 | tf_op jit(solution)/shard_map/ppermute | solution.py:17
  13.6 5.1 %collective-permute-done.4 = f32[64,1,256]{0,2,1:T(8,128)S(1)} collective-permute-done((f32[64,1,256]{0,2,1:T(8,128)S(1)}, f32[64,1,256]{0,2,1:T(8,128)S(1)}, u32[]{:S(2)}, u32[]{:S(2)}) %collective-permute-start.4) | collective-permute-done | bytes 65568 | tf_op jit(solution)/shard_map/ppermute | solution.py:17
  19.5 4.3 %collective-permute-start.5 = (f32[64,1,256]{0,2,1:T(8,128)S(1)}, f32[64,1,256]{0,2,1:T(8,128)S(1)}, u32[]{:S(2)}, u32[]{:S(2)}) collective-permute-start(f32[64,1,256]{0,2,1:T(8,128)S(1)} %get-tuple-element.43), channel_id=1, source_target_pairs={{0,2},{2,4},{4,6},{1,3},{3,5},{5,7},{8,10},{10,12},{12,14},{9,11},... | collective-permute-start | bytes 196616 | tf_op jit(solution)/shard_map/ppermute | solution.py:17
  29.7 4.8 %collective-permute-done.8 = f32[64,1,256]{0,2,1:T(8,128)S(1)} collective-permute-done((f32[64,1,256]{0,2,1:T(8,128)S(1)}, f32[64,1,256]{0,2,1:T(8,128)S(1)}, u32[]{:S(2)}, u32[]{:S(2)}) %collective-permute-start.8) | collective-permute-done | bytes 65568 | tf_op jit(solution)/shard_map/ppermute | solution.py:17
  34.6 4.8 %collective-permute-start.9 = (f32[64,1,256]{0,2,1:T(8,128)S(1)}, f32[64,1,256]{0,2,1:T(8,128)S(1)}, u32[]{:S(2)}, u32[]{:S(2)}) collective-permute-start(f32[64,1,256]{0,2,1:T(8,128)S(1)} %get-tuple-element.41), channel_id=1, source_target_pairs={{0,2},{2,4},{4,6},{1,3},{3,5},{5,7},{8,10},{10,12},{12,14},{9,11},... | collective-permute-start | bytes 196616 | tf_op jit(solution)/shard_map/ppermute | solution.py:17
  44.5 4.8 %collective-permute-done.12 = f32[64,1,256]{0,2,1:T(8,128)S(1)} collective-permute-done((f32[64,1,256]{0,2,1:T(8,128)S(1)}, f32[64,1,256]{0,2,1:T(8,128)S(1)}, u32[]{:S(2)}, u32[]{:S(2)}) %collective-permute-start.12) | collective-permute-done | bytes 65568 | tf_op jit(solution)/shard_map/ppermute | solution.py:17
  49.5 4.8 %collective-permute-start.13 = (f32[64,1,256]{0,2,1:T(8,128)S(1)}, f32[64,1,256]{0,2,1:T(8,128)S(1)}, u32[]{:S(2)}, u32[]{:S(2)}) collective-permute-start(f32[64,1,256]{0,2,1:T(8,128)S(1)} %get-tuple-element.39), channel_id=1, source_target_pairs={{0,2},{2,4},{4,6},{1,3},{3,5},{5,7},{8,10},{10,12},{12,14},{9,11},... | collective-permute-start | bytes 196616 | tf_op jit(solution)/shard_map/ppermute | solution.py:17
  59.1 4.9 %all-to-all-start = ((f32[4,1,4096]{2,1,0:T(1,128)}), f32[4,1,4096]{2,1,0:T(1,128)S(1)}, u32[]{:S(2)}, u32[]{:S(2)}) async-start(f32[4,1,4096]{2,1,0:T(1,128)} %reshape.169), calls=%async_computation | async-start | bytes 131072 | tf_op jit(solution)/shard_map/all_to_all | solution.py:111
  65.0 4.7 %all-to-all-done = f32[4,1,4096]{2,1,0:T(1,128)S(1)} async-done(((f32[4,1,4096]{2,1,0:T(1,128)}), f32[4,1,4096]{2,1,0:T(1,128)S(1)}, u32[]{:S(2)}, u32[]{:S(2)}) %all-to-all-start) | async-done | bytes 65568 | tf_op jit(solution)/shard_map/all_to_all | solution.py:111
  69.7 3.3 %all-to-all-start.2 = ((f32[4,1,4096]{2,1,0:T(1,128)}), f32[4,1,4096]{2,1,0:T(1,128)S(1)}, u32[]{:S(2)}, u32[]{:S(2)}) async-start(f32[4,1,4096]{2,1,0:T(1,128)} %reshape.167), calls=%async_computation.2 | async-start | bytes 131072 | tf_op jit(solution)/shard_map/all_to_all | solution.py:118
  75.1 3.6 %all-to-all-done.2 = f32[4,1,4096]{2,1,0:T(1,128)S(1)} async-done(((f32[4,1,4096]{2,1,0:T(1,128)}), f32[4,1,4096]{2,1,0:T(1,128)S(1)}, u32[]{:S(2)}, u32[]{:S(2)}) %all-to-all-start.2) | async-done | bytes 65568 | tf_op jit(solution)/shard_map/all_to_all | solution.py:118
  78.7 3.3 %all-to-all-start.4 = ((f32[4,1,4096]{2,1,0:T(1,128)}), f32[4,1,4096]{2,1,0:T(1,128)S(1)}, u32[]{:S(2)}, u32[]{:S(2)}) async-start(f32[4,1,4096]{2,1,0:T(1,128)} %reshape.165), calls=%async_computation.4 | async-start | bytes 131072 | tf_op jit(solution)/shard_map/all_to_all | solution.py:125
  83.7 4.0 %all-to-all-done.4 = f32[4,1,4096]{2,1,0:T(1,128)S(1)} async-done(((f32[4,1,4096]{2,1,0:T(1,128)}), f32[4,1,4096]{2,1,0:T(1,128)S(1)}, u32[]{:S(2)}, u32[]{:S(2)}) %all-to-all-start.4) | async-done | bytes 65568 | tf_op jit(solution)/shard_map/all_to_all | solution.py:125
  87.7 6.7 %all-to-all-start.1 = ((f32[256,1,1,4,16]{0,4,2,1,3:T(8,128)}), f32[256,1,1,4,16]{0,4,2,1,3:T(8,128)S(1)}, u32[]{:S(2)}, u32[]{:S(2)}) async-start(f32[256,1,1,4,16]{0,4,2,1,3:T(8,128)} %bitcast.6), calls=%async_computation.1 | async-start | bytes 131072 | tf_op jit(solution)/shard_map/all_to_all | solution.py:110
  96.2 3.1 %all-to-all-done.1 = f32[256,1,1,4,16]{0,4,2,1,3:T(8,128)S(1)} async-done(((f32[256,1,1,4,16]{0,4,2,1,3:T(8,128)}), f32[256,1,1,4,16]{0,4,2,1,3:T(8,128)S(1)}, u32[]{:S(2)}, u32[]{:S(2)}) %all-to-all-start.1) | async-done | bytes 65568 | tf_op jit(solution)/shard_map/all_to_all | solution.py:110
  99.3 3.3 %all-to-all-start.3 = ((f32[256,1,1,4,16]{0,4,2,1,3:T(8,128)}), f32[256,1,1,4,16]{0,4,2,1,3:T(8,128)S(1)}, u32[]{:S(2)}, u32[]{:S(2)}) async-start(f32[256,1,1,4,16]{0,4,2,1,3:T(8,128)} %bitcast.12), calls=%async_computation.3 | async-start | bytes 131072 | tf_op jit(solution)/shard_map/all_to_all | solution.py:117
  103.5 3.9 %all-to-all-done.3 = f32[256,1,1,4,16]{0,4,2,1,3:T(8,128)S(1)} async-done(((f32[256,1,1,4,16]{0,4,2,1,3:T(8,128)}), f32[256,1,1,4,16]{0,4,2,1,3:T(8,128)S(1)}, u32[]{:S(2)}, u32[]{:S(2)}) %all-to-all-start.3) | async-done | bytes 65568 | tf_op jit(solution)/shard_map/all_to_all | solution.py:117
  107.4 3.3 %all-to-all-start.5 = ((f32[256,1,1,4,16]{0,4,2,1,3:T(8,128)}), f32[256,1,1,4,16]{0,4,2,1,3:T(8,128)S(1)}, u32[]{:S(2)}, u32[]{:S(2)}) async-start(f32[256,1,1,4,16]{0,4,2,1,3:T(8,128)} %bitcast.18), calls=%async_computation.5 | async-start | bytes 131072 | tf_op jit(solution)/shard_map/all_to_all | solution.py:124
  111.3 4.2 %all-to-all-done.5 = f32[256,1,1,4,16]{0,4,2,1,3:T(8,128)S(1)} async-done(((f32[256,1,1,4,16]{0,4,2,1,3:T(8,128)}), f32[256,1,1,4,16]{0,4,2,1,3:T(8,128)S(1)}, u32[]{:S(2)}, u32[]{:S(2)}) %all-to-all-start.5) | async-done | bytes 65568 | tf_op jit(solution)/shard_map/all_to_all | solution.py:124
  115.6 47.1 %gather_fusion = f32[4096,256]{1,0:T(8,128)} fusion(f32[2,256,96]{1,2,0:T(8,128)S(1)} %get-tuple-element.36, s32[4096]{0:T(1024)S(1)} %bitcast.189), kind=kCustom, calls=%fused_computation | custom fusion | bytes 8421376 | tf_op jit(solution)/shard_map/vmap()/gather | solution.py:33
  162.7 5.2 %reshape.144 = f32[256,2,512,4]{0,3,2,1:T(4,128)} reshape(f32[256,2,2048]{0,2,1:T(8,128)} %bitcast.190) | data formatting | bytes 8388608 | tf_op jit(solution)/shard_map/reshape | solution.py:35
  196.7 3.2 %all-to-all-start.12 = ((f32[3,4,16]{2,0,1:T(4,128)}), f32[3,4,16]{2,0,1:T(4,128)S(1)}, u32[]{:S(2)}, u32[]{:S(2)}) async-start(f32[3,4,16]{2,0,1:T(4,128)} %copy.123), calls=%async_computation.12 | async-start | bytes 16384 | tf_op jit(solution)/shard_map/all_to_all | solution.py:169
  204.6 3.3 %all-to-all-start.8 = ((f32[4,1,4096]{2,1,0:T(1,128)}), f32[4,1,4096]{2,1,0:T(1,128)S(1)}, u32[]{:S(2)}, u32[]{:S(2)}) async-start(f32[4,1,4096]{2,1,0:T(1,128)} %reshape.175), calls=%async_computation.8 | async-start | bytes 131072 | tf_op jit(solution)/shard_map/all_to_all | solution.py:150
  208.8 4.8 %all-to-all-done.8 = f32[4,1,4096]{2,1,0:T(1,128)S(1)} async-done(((f32[4,1,4096]{2,1,0:T(1,128)}), f32[4,1,4096]{2,1,0:T(1,128)S(1)}, u32[]{:S(2)}, u32[]{:S(2)}) %all-to-all-start.8) | async-done | bytes 65568 | tf_op jit(solution)/shard_map/all_to_all | solution.py:150
  213.6 3.3 %all-to-all-start.10 = ((f32[4,1,4096]{2,1,0:T(1,128)}), f32[4,1,4096]{2,1,0:T(1,128)S(1)}, u32[]{:S(2)}, u32[]{:S(2)}) async-start(f32[4,1,4096]{2,1,0:T(1,128)} %reshape.179), calls=%async_computation.10 | async-start | bytes 131072 | tf_op jit(solution)/shard_map/all_to_all | solution.py:157
  218.2 4.4 %all-to-all-done.10 = f32[4,1,4096]{2,1,0:T(1,128)S(1)} async-done(((f32[4,1,4096]{2,1,0:T(1,128)}), f32[4,1,4096]{2,1,0:T(1,128)S(1)}, u32[]{:S(2)}, u32[]{:S(2)}) %all-to-all-start.10) | async-done | bytes 65568 | tf_op jit(solution)/shard_map/all_to_all | solution.py:157
  222.6 3.3 %all-to-all-start.6 = ((f32[4,1,4096]{2,1,0:T(1,128)}), f32[4,1,4096]{2,1,0:T(1,128)S(1)}, u32[]{:S(2)}, u32[]{:S(2)}) async-start(f32[4,1,4096]{2,1,0:T(1,128)} %reshape.171), calls=%async_computation.6 | async-start | bytes 131072 | tf_op jit(solution)/shard_map/all_to_all | solution.py:143
  228.0 3.6 %all-to-all-done.6 = f32[4,1,4096]{2,1,0:T(1,128)S(1)} async-done(((f32[4,1,4096]{2,1,0:T(1,128)}), f32[4,1,4096]{2,1,0:T(1,128)S(1)}, u32[]{:S(2)}, u32[]{:S(2)}) %all-to-all-start.6) | async-done | bytes 65568 | tf_op jit(solution)/shard_map/all_to_all | solution.py:143
  231.6 3.6 %all-to-all-start.9 = ((f32[4,1,4096]{2,1,0:T(1,128)}), f32[4,1,4096]{2,1,0:T(1,128)S(1)}, u32[]{:S(2)}, u32[]{:S(2)}) async-start(f32[4,1,4096]{2,1,0:T(1,128)} %reshape.177), calls=%async_computation.9 | async-start | bytes 131072 | tf_op jit(solution)/shard_map/all_to_all | solution.py:149
  240.0 3.3 %all-to-all-start.11 = ((f32[4,1,4096]{2,1,0:T(1,128)}), f32[4,1,4096]{2,1,0:T(1,128)S(1)}, u32[]{:S(2)}, u32[]{:S(2)}) async-start(f32[4,1,4096]{2,1,0:T(1,128)} %reshape.181), calls=%async_computation.11 | async-start | bytes 131072 | tf_op jit(solution)/shard_map/all_to_all | solution.py:156
  244.2 4.0 %all-to-all-done.11 = f32[4,1,4096]{2,1,0:T(1,128)S(1)} async-done(((f32[4,1,4096]{2,1,0:T(1,128)}), f32[4,1,4096]{2,1,0:T(1,128)S(1)}, u32[]{:S(2)}, u32[]{:S(2)}) %all-to-all-start.11) | async-done | bytes 65568 | tf_op jit(solution)/shard_map/all_to_all | solution.py:156
  248.1 3.3 %all-to-all-start.7 = ((f32[4,1,4096]{2,1,0:T(1,128)}), f32[4,1,4096]{2,1,0:T(1,128)S(1)}, u32[]{:S(2)}, u32[]{:S(2)}) async-start(f32[4,1,4096]{2,1,0:T(1,128)} %reshape.173), calls=%async_computation.7 | async-start | bytes 131072 | tf_op jit(solution)/shard_map/all_to_all | solution.py:142
  (185 shorter events, 82.2 us)
Async XLA Ops:
  0.6 33.8 %copy-start.1 = (f32[1,256]{1,0:T(1,128)S(1)}, f32[1,256]{1,0:T(1,128)}, u32[]{:S(2)}) copy-start(f32[1,256]{1,0:T(1,128)} %param.15) | copy-start | bytes 3076
  0.7 53.7 %copy-start.3 = (s32[2,512,4]{1,2,0:T(4,128)S(1)}, s32[2,512,4]{1,2,0:T(4,128)}, u32[]{:S(2)}) copy-start(s32[2,512,4]{1,2,0:T(4,128)} %param.16) | copy-start | bytes 49156
  2.4 7.8 %collective-permute-start.1 = (f32[64,1,256]{0,2,1:T(8,128)S(1)}, f32[64,1,256]{0,2,1:T(8,128)S(1)}, u32[]{:S(2)}, u32[]{:S(2)}) collective-permute-start(f32[64,1,256]{0,2,1:T(8,128)S(1)} %broadcast_multiply_fusion.3), channel_id=1, source_target_pairs={{0,2},{2,4},{4,6},{1,3},{3,5},{5,7},{8,10},{10,12},{12,14},{9,11},... | collective-permute-start | bytes 196616 | tf_op jit(solution)/shard_map/ppermute | solution.py:17
  9.0 1.2 collective-permute-start
  11.1 7.6 %collective-permute-start.4 = (f32[64,1,256]{0,2,1:T(8,128)S(1)}, f32[64,1,256]{0,2,1:T(8,128)S(1)}, u32[]{:S(2)}, u32[]{:S(2)}) collective-permute-start(f32[64,1,256]{0,2,1:T(8,128)S(1)} %fusion.34), channel_id=1, source_target_pairs={{2,0},{4,2},{6,4},{3,1},{5,3},{7,5},{10,8},{12,10},{14,12},{11,9},... | collective-permute-start | bytes 196616 | tf_op jit(solution)/shard_map/ppermute | solution.py:17
  12.4 1.2 collective-permute-start.2
  19.5 6.8 %collective-permute-start.5 = (f32[64,1,256]{0,2,1:T(8,128)S(1)}, f32[64,1,256]{0,2,1:T(8,128)S(1)}, u32[]{:S(2)}, u32[]{:S(2)}) collective-permute-start(f32[64,1,256]{0,2,1:T(8,128)S(1)} %get-tuple-element.43), channel_id=1, source_target_pairs={{0,2},{2,4},{4,6},{1,3},{3,5},{5,7},{8,10},{10,12},{12,14},{9,11},... | collective-permute-start | bytes 196616 | tf_op jit(solution)/shard_map/ppermute | solution.py:17
  23.9 1.2 collective-permute-start.3
  27.1 7.3 %collective-permute-start.8 = (f32[64,1,256]{0,2,1:T(8,128)S(1)}, f32[64,1,256]{0,2,1:T(8,128)S(1)}, u32[]{:S(2)}, u32[]{:S(2)}) collective-permute-start(f32[64,1,256]{0,2,1:T(8,128)S(1)} %fusion.38), channel_id=1, source_target_pairs={{2,0},{4,2},{6,4},{3,1},{5,3},{7,5},{10,8},{12,10},{14,12},{11,9},... | collective-permute-start | bytes 196616 | tf_op jit(solution)/shard_map/ppermute | solution.py:17
  28.4 1.2 collective-permute-start.6
  34.6 7.3 %collective-permute-start.9 = (f32[64,1,256]{0,2,1:T(8,128)S(1)}, f32[64,1,256]{0,2,1:T(8,128)S(1)}, u32[]{:S(2)}, u32[]{:S(2)}) collective-permute-start(f32[64,1,256]{0,2,1:T(8,128)S(1)} %get-tuple-element.41), channel_id=1, source_target_pairs={{0,2},{2,4},{4,6},{1,3},{3,5},{5,7},{8,10},{10,12},{12,14},{9,11},... | collective-permute-start | bytes 196616 | tf_op jit(solution)/shard_map/ppermute | solution.py:17
  39.4 1.2 collective-permute-start.7
  42.0 7.3 %collective-permute-start.12 = (f32[64,1,256]{0,2,1:T(8,128)S(1)}, f32[64,1,256]{0,2,1:T(8,128)S(1)}, u32[]{:S(2)}, u32[]{:S(2)}) collective-permute-start(f32[64,1,256]{0,2,1:T(8,128)S(1)} %fusion.42), channel_id=1, source_target_pairs={{2,0},{4,2},{6,4},{3,1},{5,3},{7,5},{10,8},{12,10},{14,12},{11,9},... | collective-permute-start | bytes 196616 | tf_op jit(solution)/shard_map/ppermute | solution.py:17
  43.3 1.2 collective-permute-start.10
  49.4 61.3 %copy-start.4 = (f32[2,512,4]{1,2,0:T(4,128)S(1)}, f32[2,512,4]{1,2,0:T(4,128)}, u32[]{:S(2)}) copy-start(f32[2,512,4]{1,2,0:T(4,128)} %param.17) | copy-start | bytes 49156
  49.5 7.3 %collective-permute-start.13 = (f32[64,1,256]{0,2,1:T(8,128)S(1)}, f32[64,1,256]{0,2,1:T(8,128)S(1)}, u32[]{:S(2)}, u32[]{:S(2)}) collective-permute-start(f32[64,1,256]{0,2,1:T(8,128)S(1)} %get-tuple-element.39), channel_id=1, source_target_pairs={{0,2},{2,4},{4,6},{1,3},{3,5},{5,7},{8,10},{10,12},{12,14},{9,11},... | collective-permute-start | bytes 196616 | tf_op jit(solution)/shard_map/ppermute | solution.py:17
  54.3 1.2 collective-permute-start.11
  56.9 7.3 %collective-permute-start.15 = (f32[64,1,256]{0,2,1:T(8,128)S(1)}, f32[64,1,256]{0,2,1:T(8,128)S(1)}, u32[]{:S(2)}, u32[]{:S(2)}) collective-permute-start(f32[64,1,256]{0,2,1:T(8,128)S(1)} %fusion.46), channel_id=1, source_target_pairs={{2,0},{4,2},{6,4},{3,1},{5,3},{7,5},{10,8},{12,10},{14,12},{11,9},... | collective-permute-start | bytes 196616 | tf_op jit(solution)/shard_map/ppermute | solution.py:17
  58.2 5.7 %collective-permute-start.14 = (f32[64,1,1]{0,2,1:T(1,128)S(1)}, f32[64,1,1]{0,2,1:T(1,128)S(1)}, u32[]{:S(2)}, u32[]{:S(2)}) collective-permute-start(f32[64,1,1]{0,2,1:T(1,128)S(1)} %slice.93), channel_id=1, source_target_pairs={{1,0},{0,1},{3,2},{2,3},{5,4},{4,5},{7,6},{6,7},{9,8},{8,9},{11,10... | collective-permute-start | bytes 776 | tf_op jit(solution)/shard_map/ppermute | solution.py:23
  59.1 10.6 %all-to-all-start = ((f32[4,1,4096]{2,1,0:T(1,128)}), f32[4,1,4096]{2,1,0:T(1,128)S(1)}, u32[]{:S(2)}, u32[]{:S(2)}) async-start(f32[4,1,4096]{2,1,0:T(1,128)} %reshape.169), calls=%async_computation | async-start | bytes 131072 | tf_op jit(solution)/shard_map/all_to_all | solution.py:111
  69.7 9.0 %all-to-all-start.2 = ((f32[4,1,4096]{2,1,0:T(1,128)}), f32[4,1,4096]{2,1,0:T(1,128)S(1)}, u32[]{:S(2)}, u32[]{:S(2)}) async-start(f32[4,1,4096]{2,1,0:T(1,128)} %reshape.167), calls=%async_computation.2 | async-start | bytes 131072 | tf_op jit(solution)/shard_map/all_to_all | solution.py:118
  78.7 9.0 %all-to-all-start.4 = ((f32[4,1,4096]{2,1,0:T(1,128)}), f32[4,1,4096]{2,1,0:T(1,128)S(1)}, u32[]{:S(2)}, u32[]{:S(2)}) async-start(f32[4,1,4096]{2,1,0:T(1,128)} %reshape.165), calls=%async_computation.4 | async-start | bytes 131072 | tf_op jit(solution)/shard_map/all_to_all | solution.py:125
  87.7 11.6 %all-to-all-start.1 = ((f32[256,1,1,4,16]{0,4,2,1,3:T(8,128)}), f32[256,1,1,4,16]{0,4,2,1,3:T(8,128)S(1)}, u32[]{:S(2)}, u32[]{:S(2)}) async-start(f32[256,1,1,4,16]{0,4,2,1,3:T(8,128)} %bitcast.6), calls=%async_computation.1 | async-start | bytes 131072 | tf_op jit(solution)/shard_map/all_to_all | solution.py:110
  99.3 8.1 %all-to-all-start.3 = ((f32[256,1,1,4,16]{0,4,2,1,3:T(8,128)}), f32[256,1,1,4,16]{0,4,2,1,3:T(8,128)S(1)}, u32[]{:S(2)}, u32[]{:S(2)}) async-start(f32[256,1,1,4,16]{0,4,2,1,3:T(8,128)} %bitcast.12), calls=%async_computation.3 | async-start | bytes 131072 | tf_op jit(solution)/shard_map/all_to_all | solution.py:117
  107.4 8.1 %all-to-all-start.5 = ((f32[256,1,1,4,16]{0,4,2,1,3:T(8,128)}), f32[256,1,1,4,16]{0,4,2,1,3:T(8,128)S(1)}, u32[]{:S(2)}, u32[]{:S(2)}) async-start(f32[256,1,1,4,16]{0,4,2,1,3:T(8,128)} %bitcast.18), calls=%async_computation.5 | async-start | bytes 131072 | tf_op jit(solution)/shard_map/all_to_all | solution.py:124
  196.7 7.9 %all-to-all-start.12 = ((f32[3,4,16]{2,0,1:T(4,128)}), f32[3,4,16]{2,0,1:T(4,128)S(1)}, u32[]{:S(2)}, u32[]{:S(2)}) async-start(f32[3,4,16]{2,0,1:T(4,128)} %copy.123), calls=%async_computation.12 | async-start | bytes 16384 | tf_op jit(solution)/shard_map/all_to_all | solution.py:169
  204.6 9.0 %all-to-all-start.8 = ((f32[4,1,4096]{2,1,0:T(1,128)}), f32[4,1,4096]{2,1,0:T(1,128)S(1)}, u32[]{:S(2)}, u32[]{:S(2)}) async-start(f32[4,1,4096]{2,1,0:T(1,128)} %reshape.175), calls=%async_computation.8 | async-start | bytes 131072 | tf_op jit(solution)/shard_map/all_to_all | solution.py:150
  213.6 9.0 %all-to-all-start.10 = ((f32[4,1,4096]{2,1,0:T(1,128)}), f32[4,1,4096]{2,1,0:T(1,128)S(1)}, u32[]{:S(2)}, u32[]{:S(2)}) async-start(f32[4,1,4096]{2,1,0:T(1,128)} %reshape.179), calls=%async_computation.10 | async-start | bytes 131072 | tf_op jit(solution)/shard_map/all_to_all | solution.py:157
  222.6 9.0 %all-to-all-start.6 = ((f32[4,1,4096]{2,1,0:T(1,128)}), f32[4,1,4096]{2,1,0:T(1,128)S(1)}, u32[]{:S(2)}, u32[]{:S(2)}) async-start(f32[4,1,4096]{2,1,0:T(1,128)} %reshape.171), calls=%async_computation.6 | async-start | bytes 131072 | tf_op jit(solution)/shard_map/all_to_all | solution.py:143
  231.6 8.4 %all-to-all-start.9 = ((f32[4,1,4096]{2,1,0:T(1,128)}), f32[4,1,4096]{2,1,0:T(1,128)S(1)}, u32[]{:S(2)}, u32[]{:S(2)}) async-start(f32[4,1,4096]{2,1,0:T(1,128)} %reshape.177), calls=%async_computation.9 | async-start | bytes 131072 | tf_op jit(solution)/shard_map/all_to_all | solution.py:149
  240.0 8.1 %all-to-all-start.11 = ((f32[4,1,4096]{2,1,0:T(1,128)}), f32[4,1,4096]{2,1,0:T(1,128)S(1)}, u32[]{:S(2)}, u32[]{:S(2)}) async-start(f32[4,1,4096]{2,1,0:T(1,128)} %reshape.181), calls=%async_computation.11 | async-start | bytes 131072 | tf_op jit(solution)/shard_map/all_to_all | solution.py:156
  248.1 8.1 %all-to-all-start.7 = ((f32[4,1,4096]{2,1,0:T(1,128)}), f32[4,1,4096]{2,1,0:T(1,128)S(1)}, u32[]{:S(2)}, u32[]{:S(2)}) async-start(f32[4,1,4096]{2,1,0:T(1,128)} %reshape.173), calls=%async_computation.7 | async-start | bytes 131072 | tf_op jit(solution)/shard_map/all_to_all | solution.py:142
  (6 other events, 63.3 us)
where the time goes:
time: 260 us; the launch traced here: 258 us
  local copies, waits for them, and re-layouts  74.7 us (29%)
  starting transfers between devices  72.9 us (28%)
  waiting for transfers between devices  70.3 us (27%)
  matrix products  20.5 us (8%)
  other arithmetic  17.9 us (7%)
    gather x1, local copies, waits for them, and re-layouts, analyse_regions(): column_block[:, positions]  47.1 us
    ppermute x8, starting transfers between devices, shifted(): return lax.ppermute(shard, axis, pairs)  24 us
    ppermute x8, waiting for transfers between devices, shifted(): return lax.ppermute(shard, axis, pairs)  18.6 us
    unnamed x48, local copies, waits for them, and re-layouts  15.5 us
    all_to_all x1, starting transfers between devices, shards(): lax.all_to_all(lax.all_to_all(view_h, 'member', split_axis=2, concat_axis...  6.72 us
    ppermute x8, waiting for transfers between devices, passed_along(): return lax.ppermute(block, axis, route)  6.19 us
    dot_general x8, matrix products, analyse_regions(): jnp.einsum('rij,rjk->rik', factor, inverse_root, precision=HIGHEST)  5.42 us
    dot_general x8, matrix products, analyse_regions(): jnp.einsum('rij,rjk->rik', inverse_root, iterate, precision=HIGHEST)  5.33 us
  transfers between devices with their start and end apart: 29, of which 27 were waited for; matrix products, arithmetic and copies ran while one was open for 9% of the time, Pallas kernels for 0%

commit v1 on v0

v1 whole, which is shorter than its diff:
```python
import functools

import jax
import jax.numpy as jnp
from jax import lax
from jax.experimental import pallas as pl
from jax.experimental.pallas import tpu as pltpu
from jax.sharding import PartitionSpec as P

REG_DEV = 2
STEPS = 4
NEWTON = 8
LANES = 128
TILE = 8
HALF = LANES // 2

HIGHEST = lax.Precision.HIGHEST
NT = (((1,), (1,)), ((), ()))
NN = (((1,), (0,)), ((), ()))
VMEM = pl.BlockSpec(memory_space=pltpu.VMEM)
SMEM = pl.BlockSpec(memory_space=pltpu.SMEM)


def passed_along(block, axis, distance):
    count = lax.axis_size(axis)
    route = [((i - distance) % count, i) for i in range(count)]
    return lax.ppermute(block, axis, route)


def lane_of(shape):
    return lax.broadcasted_iota(jnp.int32, shape, 1)


def row_of(shape):
    return lax.broadcasted_iota(jnp.int32, shape, 0)


def swapped(tile):
    return pltpu.roll(tile, HALF, 1)


def low_pair(even, odd):
    return jnp.where(lane_of(even.shape) < HALF, even, swapped(odd))


def high_pair(even, odd):
    return jnp.where(lane_of(even.shape) < HALF, swapped(even), odd)


def split(value):
    high = value.astype(jnp.bfloat16)
    return high, (value - high.astype(jnp.float32)).astype(jnp.bfloat16)


def product(left, right, dims=NN):
    left_high, left_low = split(left)
    right_high, right_low = split(right)
    dot = functools.partial(
        lax.dot_general, dimension_numbers=dims, preferred_element_type=jnp.float32
    )
    return dot(left_high, right_high) + (dot(left_high, right_low) + dot(left_low, right_high))


OUT_ROWS = 5 * TILE
BACK_ROWS = 4 * TILE


def turn_kernel(mem, h_ref, u_ref, v_ref, zonal_ref, merid_ref, pair_ref, single_ref, edge_ref):
    tiles = h_ref.shape[0] // mem
    columns = tiles * LANES
    zero = jnp.zeros((TILE, LANES), jnp.float32)
    for ref in (pair_ref, single_ref):
        ref[0:TILE, :] = zero
        ref[columns : columns + TILE, :] = zero
    for t in range(tiles):
        rows = pl.ds(t, mem, stride=tiles)
        lanes = slice(t * LANES, (t + 1) * LANES)
        pair = jnp.concatenate([h_ref[rows, :], u_ref[rows, :]], axis=0)
        zonal = jnp.broadcast_to(zonal_ref[:, lanes], (mem // 2, LANES))
        merid = jnp.broadcast_to(merid_ref[:, lanes], (mem // 2, LANES))
        single = jnp.concatenate([v_ref[rows, :], zonal, merid], axis=0)
        place = slice(STEPS + t * LANES, STEPS + (t + 1) * LANES)
        pair_ref[place, :] = pair.T
        single_ref[place, :] = single.T
    early = row_of((TILE, LANES)) < STEPS
    for i, ref in enumerate((pair_ref, single_ref)):
        edge_ref[i] = jnp.where(early, ref[columns : columns + TILE, :], ref[0:TILE, :])


def blocks_kernel(width, pair_ref, single_ref, west_ref, east_ref, send_ref):
    count = send_ref.shape[0]
    shape = (TILE, LANES)
    early = row_of(shape) < STEPS
    lane = lane_of(shape)
    low = lane < HALF
    part = lane % (HALF // 2)
    for d in range(count):
        pair = [pair_ref[width * d + TILE * j : width * d + TILE * (j + 1), :] for j in range(3)]
        single = [
            single_ref[width * d + TILE * j : width * d + TILE * (j + 1), :] for j in range(3)
        ]
        if d == 0:
            pair[0] = jnp.where(early, west_ref[0], pair[0])
            single[0] = jnp.where(early, west_ref[1], single[0])
        if d == count - 1:
            pair[2] = jnp.where(early, pair[2], east_ref[0])
            single[2] = jnp.where(early, single[2], east_ref[1])
        for j in range(3):
            send_ref[d, TILE * j : TILE * (j + 1), :] = pair[j]
        courant = jnp.where(part == 0, single[0], jnp.where(part == 1, single[1], single[2]))
        send_ref[d, 3 * TILE : 4 * TILE, :] = jnp.where(low, single[0], swapped(single[1]))
        send_ref[d, 4 * TILE : 5 * TILE, :] = jnp.where(low, single[2], courant)


def forecast(groups, strips, width, got_ref, x_ref):
    span = width + 2 * STEPS
    per_region = strips // REG_DEV
    cells = per_region * width

    def tiles_of(group, strip):
        block = group * strips + strip
        return [got_ref[block, TILE * j : TILE * (j + 1), :] for j in range(5)]

    zonal, merid = [], []
    for r in range(strips):
        mixed = got_ref[r, 4 * TILE : 5 * TILE, :]

        def column(first):
            parts = [
                jnp.broadcast_to(mixed[:, first + j : first + j + 1], (TILE, LANES))
                for j in range(3)
            ]
            return jnp.concatenate(parts, axis=0)

        zonal.append(column(HALF))
        merid.append(column(HALF + HALF // 2))
    for lane_tile in range(groups // 2):
        h, u, v = [], [], []
        for r in range(strips):
            even, odd = tiles_of(2 * lane_tile, r), tiles_of(2 * lane_tile + 1, r)
            h.append(jnp.concatenate([low_pair(even[j], odd[j]) for j in range(3)], axis=0))
            u.append(jnp.concatenate([high_pair(even[j], odd[j]) for j in range(3)], axis=0))
            v.append(
                jnp.concatenate(
                    [
                        low_pair(even[3], odd[3]),
                        high_pair(even[3], odd[3]),
                        low_pair(even[4], odd[4]),
                    ],
                    axis=0,
                )
            )
        for _ in range(STEPS):
            flux_v = [merid[r] * v[r] for r in range(strips)]
            for r in range(strips):
                flux_u = zonal[r] * u[r]
                south = flux_v[r - 1] if r else jnp.zeros_like(flux_u)
                h[r] = h[r] - (flux_u - pltpu.roll(flux_u, 1, 0) + flux_v[r] - south)
            for r in range(strips):
                north = h[r + 1] if r + 1 < strips else jnp.zeros_like(h[r])
                u[r] = u[r] - (pltpu.roll(h[r], span - 1, 0) - h[r])
                v[r] = v[r] - (north - h[r])
        lanes = slice(lane_tile * LANES, (lane_tile + 1) * LANES)
        for i, field in enumerate((h, u, v)):
            for r in range(strips):
                q, s = divmod(r, per_region)
                place = slice(i * cells + s * width, i * cells + (s + 1) * width)
                x_ref[q, place, lanes] = pltpu.roll(field[r], span - STEPS, 0)[:width]


def observe_kernel(index_ref, weight_ref, value_ref, var_ref, count_ref, info_ref, pull_ref):
    states = info_ref.shape[1]
    obs = index_ref.shape[2]
    for q in range(REG_DEV):
        state = row_of((states, obs))
        operator = jnp.zeros((states, obs), jnp.float32)
        for j in range(index_ref.shape[1]):
            hit = state == index_ref[q, j : j + 1, :]
            operator = operator + jnp.where(hit, weight_ref[q, j : j + 1, :], 0.0)
        live = lane_of((1, obs)) < count_ref[q]
        inverse = jnp.where(live, 1.0 / var_ref[q : q + 1, :], 0.0)
        scaled = operator * inverse
        info_ref[q] = lax.dot_general(
            scaled, operator, NT, precision=HIGHEST, preferred_element_type=jnp.float32
        )
        pulled = jnp.sum(scaled * value_ref[q : q + 1, :], axis=1, keepdims=True)
        pull_ref[q] = jnp.broadcast_to(pulled, (states, LANES))


def analyse(members, x_ref, info_ref, pull_ref, out_ref):
    states = x_ref.shape[1]
    square = (states, states)
    diagonal = row_of(square) == lane_of(square)
    identity = jnp.where(diagonal, 1.0, 0.0)
    regions = range(REG_DEV)
    scale = 1.0 / (members - 1)
    means, spreads, covs, inverses, iterates, norms = [], [], [], [], [], []
    for q in regions:
        x = x_ref[q]
        mean = jnp.sum(x, axis=1, keepdims=True) / members
        spread = x - mean
        means.append(mean)
        spreads.append(spread)
        covs.append(product(spread, spread, NT))
    for q in regions:
        info = info_ref[q]
        gain = product(covs[q], info) * scale
        gain_t = product(info, covs[q]) * scale
        total = jnp.sum(gain * gain_t + jnp.where(diagonal, 2.0 * gain, 0.0), keepdims=True)
        frobenius = jnp.sqrt(total + members)
        norms.append(frobenius)
        iterates.append((identity + gain) / frobenius)
    factors = [1.5 * identity - 0.5 * iterates[q] for q in regions]
    iterates = [product(iterates[q], factors[q]) for q in regions]
    inverses = factors
    for sweep in range(1, NEWTON):
        factors = [1.5 * identity - 0.5 * product(inverses[q], iterates[q]) for q in regions]
        if sweep < NEWTON - 1:
            iterates = [product(iterates[q], factors[q]) for q in regions]
        inverses = [product(factors[q], inverses[q]) for q in regions]
    increments = []
    for q in regions:
        root = inverses[q] / jnp.sqrt(norms[q])
        mean_row = jnp.sum(jnp.where(diagonal, means[q], 0.0), axis=0, keepdims=True)
        pulled = pull_ref[q][:, 0:1] - jnp.sum(info_ref[q] * mean_row, axis=1, keepdims=True)
        pulled = jnp.sum(covs[q] * pulled, axis=0, keepdims=True)
        shift = jnp.sum(root * pulled, axis=1, keepdims=True) * scale
        out_ref[q] = product(root, spreads[q] + shift) + means[q]
        shift_row = jnp.sum(jnp.where(diagonal, shift, 0.0), axis=0, keepdims=True)
        increments.append(jnp.sum(root * shift_row, axis=1, keepdims=True))
    return increments


def pack(groups, strips, width, ana_ref, increments, send_ref):
    per_region = strips // REG_DEV
    cells = per_region * width
    states = increments[0].shape[0]
    state = row_of((states, LANES))
    lane = lane_of((states, LANES))
    for r in range(strips):
        q, s = divmod(r, per_region)
        wanted = (lane // width) * cells + s * width + lane % width
        hit = (state == wanted) & (lane < 3 * width)
        row = jnp.sum(jnp.where(hit, increments[q], 0.0), axis=0, keepdims=True)
        row = jnp.broadcast_to(row, (TILE, LANES))
        for group in range(groups):
            block = group * strips + r
            lanes = slice((group // 2) * LANES, (group // 2 + 1) * LANES)
            pair = high_pair if group % 2 else low_pair
            for i in range(3):
                first = i * cells + s * width
                tile = pair(
                    ana_ref[q, first : first + TILE, lanes],
                    ana_ref[q, first + TILE : first + 2 * TILE, lanes],
                )
                send_ref[block, TILE * i : TILE * (i + 1), :] = tile
            send_ref[block, 3 * TILE : 4 * TILE, :] = row


def region_kernel(groups, strips, width, got_ref, info_ref, pull_ref, send_ref, x_ref, ana_ref):
    states = 3 * width * strips // REG_DEV
    if states < x_ref.shape[1]:
        x_ref[:, states:, :] = jnp.zeros_like(x_ref[:, states:, :])
    forecast(groups, strips, width, got_ref, x_ref)
    members = x_ref.shape[2]
    increments = analyse(members, x_ref, info_ref, pull_ref, ana_ref)
    pack(groups, strips, width, ana_ref, increments, send_ref)


def home_kernel(mem, strips, width, group_ref, got_ref, ctrl_ref, h_ref, u_ref, v_ref, fine_ref):
    blocks = got_ref.shape[0]
    tiles = blocks * width // LANES
    per_tile = LANES // width
    for i, out_ref in enumerate((h_ref, u_ref, v_ref)):
        for t in range(0, tiles, 2):
            rows = []
            for k in range(per_tile):
                even = got_ref[t * per_tile + k, TILE * i : TILE * (i + 1), :]
                odd = got_ref[(t + 1) * per_tile + k, TILE * i : TILE * (i + 1), :]
                rows += [low_pair(even, odd), high_pair(even, odd)]
            turned = jnp.concatenate(rows, axis=0).T
            out_ref[pl.ds(t, mem, stride=tiles), :] = turned[:mem]
            out_ref[pl.ds(t + 1, mem, stride=tiles), :] = turned[mem:]
    mine = group_ref[0] * strips
    per_fine = LANES // (2 * width)
    row = row_of((width, LANES))
    lane = lane_of((width, LANES))
    for t in range(ctrl_ref.shape[3] // LANES):
        rows = [got_ref[mine + t * per_fine + b, 3 * TILE : 4 * TILE, :] for b in range(per_fine)]
        columns = [jnp.concatenate([r] * (LANES // TILE), axis=0).T[:, 0:1] for r in rows]
        for i in range(3):
            total = jnp.zeros((1, LANES), jnp.float32)
            for b in range(per_fine):
                hit = ((lane // 2) % width == row) & (lane // (2 * width) == b)
                part = jnp.where(hit, columns[b][i * width : (i + 1) * width], 0.0)
                total = total + jnp.sum(part, axis=0, keepdims=True)
            lanes = slice(t * LANES, (t + 1) * LANES)
            for e in range(2):
                fine_ref[i, e, :, lanes] = ctrl_ref[i, e, :, lanes] + total


def forecast_kernel(groups, strips, width, got_ref, x_ref):
    forecast(groups, strips, width, got_ref, x_ref)


def pack_kernel(groups, strips, width, ana_ref, inc_ref, send_ref):
    pack(groups, strips, width, ana_ref, [inc_ref[q] for q in range(REG_DEV)], send_ref)


def analyse_in_members(x, obs_index, obs_weight, obs_value, obs_var, obs_count):
    states, members = x.shape[1:]
    mean_state = jnp.mean(x, axis=2, keepdims=True)
    spread = x - mean_state
    picks = (obs_index[:, :, :, None] == jnp.arange(states)).astype(jnp.float32)
    operator = jnp.sum(picks * obs_weight[:, :, :, None], axis=2)
    predicted = jnp.einsum("ros,rsk->rko", operator, x, precision=HIGHEST)
    mean_obs = jnp.mean(predicted, axis=1, keepdims=True)
    obs_spread = predicted - mean_obs
    active_obs = jnp.arange(obs_value.shape[1])[None, :] < obs_count[:, None]
    weighted = obs_spread * (active_obs.astype(jnp.float32) / obs_var)[:, None, :]
    gram_sum = jnp.einsum("rko,rjo->rkj", weighted, obs_spread, precision=HIGHEST)
    identity = jnp.eye(members, dtype=jnp.float32)
    scaled = identity + gram_sum / (members - 1)
    frobenius = jnp.sqrt(jnp.sum(scaled * scaled, axis=(1, 2), keepdims=True))
    iterate = scaled / frobenius
    inverse_root = jnp.broadcast_to(identity, scaled.shape)
    dot = functools.partial(jnp.einsum, "rij,rjk->rik", precision=HIGHEST)
    for _ in range(NEWTON):
        factor = 1.5 * identity - 0.5 * dot(inverse_root, iterate)
        iterate = dot(iterate, factor)
        inverse_root = dot(factor, inverse_root)
    transform = inverse_root / jnp.sqrt(frobenius)
    innovation = jnp.einsum(
        "rko,ro->rk", weighted, obs_value - mean_obs[:, 0], precision=HIGHEST
    )
    halfway = jnp.einsum("rkj,rj->rk", transform, innovation, precision=HIGHEST)
    mean_weights = jnp.einsum("rkj,rj->rk", transform, halfway, precision=HIGHEST) / (members - 1)
    increment = jnp.einsum("rk,rsk->rs", mean_weights, spread, precision=HIGHEST)[:, :, None]
    moved = jnp.einsum("rjk,rsj->rsk", transform, spread, precision=HIGHEST)
    return mean_state + increment + moved, increment


def call(kernel, out_shape, specs, scratch=(), cost=None, name=None):
    return pl.pallas_call(
        kernel,
        out_shape=out_shape,
        in_specs=specs,
        out_specs=jax.tree.map(lambda _: VMEM, out_shape),
        scratch_shapes=scratch,
        cost_estimate=cost,
        name=name,
    )


def f32(*shape):
    return jax.ShapeDtypeStruct(shape, jnp.float32)


def shards(
    sample_surface_elevation,
    sample_zonal_current,
    sample_meridional_current,
    zonal_edge_layer_courant,
    meridional_edge_layer_courant,
    obs_index,
    obs_weight,
    obs_value,
    obs_var,
    obs_count,
    fine_ctrl,
):
    groups = lax.axis_size("member")
    strips = lax.axis_size("region")
    owners = ("member", "region")
    mem, rows, columns = sample_surface_elevation.shape
    count = groups * strips
    width = columns // count
    members = groups * mem
    assert rows == 1 and 2 * mem == LANES and width == 2 * TILE and STEPS * 2 == TILE
    assert columns % (2 * LANES) == 0 and groups % 2 == 0 and strips % REG_DEV == 0
    flat = (mem * columns // LANES, LANES)
    pair, single, edge = call(
        functools.partial(turn_kernel, mem),
        (f32(columns + TILE, LANES), f32(columns + TILE, LANES), f32(2, TILE, LANES)),
        [VMEM] * 5,
        name="turn",
    )(
        sample_surface_elevation.reshape(flat),
        sample_zonal_current.reshape(flat),
        sample_meridional_current.reshape(flat),
        zonal_edge_layer_courant,
        meridional_edge_layer_courant,
    )
    from_west = passed_along(edge, "fine", 1)
    from_east = from_west if lax.axis_size("fine") == 2 else passed_along(edge, "fine", -1)
    out = call(
        functools.partial(blocks_kernel, width),
        f32(count, OUT_ROWS, LANES),
        [VMEM] * 4,
        name="blocks",
    )(pair, single, from_west, from_east)
    got = lax.all_to_all(out, owners, split_axis=0, concat_axis=0, tiled=True)
    states = 3 * width * strips // REG_DEV
    back_shape = f32(count, BACK_ROWS, LANES)
    layout = (groups, strips, width)
    if states <= members:
        padded = -(-states // LANES) * LANES
        obs = obs_value.shape[1]
        info, pull = call(
            observe_kernel,
            (f32(REG_DEV, padded, padded), f32(REG_DEV, padded, LANES)),
            [VMEM] * 4 + [SMEM],
            cost=pl.CostEstimate(
                flops=12 * REG_DEV * padded * padded * obs, bytes_accessed=1 << 20, transcendentals=0
            ),
            name="observe",
        )(
            obs_index.transpose(0, 2, 1),
            obs_weight.transpose(0, 2, 1),
            obs_value,
            obs_var,
            obs_count,
        )
        back = call(
            functools.partial(region_kernel, *layout),
            back_shape,
            [VMEM] * 3,
            scratch=[
                pltpu.VMEM((REG_DEV, padded, members), jnp.float32),
                pltpu.VMEM((REG_DEV, padded, members), jnp.float32),
            ],
            name="region",
        )(got, info, pull)
    else:
        x = call(
            functools.partial(forecast_kernel, *layout),
            f32(REG_DEV, states, members),
            [VMEM],
            name="forecast",
        )(got)
        analysis, increment = analyse_in_members(
            x, obs_index, obs_weight, obs_value, obs_var, obs_count
        )
        back = call(
            functools.partial(pack_kernel, *layout), back_shape, [VMEM] * 2, name="pack"
        )(analysis, increment)
    home = lax.all_to_all(back, owners, split_axis=0, concat_axis=0, tiled=True)
    mine = lax.axis_index("member").astype(jnp.int32).reshape(1)
    ana_h, ana_u, ana_v, fine_out = call(
        functools.partial(home_kernel, mem, strips, width),
        (f32(*flat), f32(*flat), f32(*flat), f32(*fine_ctrl.shape)),
        [SMEM, VMEM, VMEM],
        name="home",
    )(mine, home, fine_ctrl)
    shape = (mem, rows, columns)
    return (ana_h.reshape(shape), ana_u.reshape(shape), ana_v.reshape(shape), fine_out)


def solution(mesh):
    strip = P("member", "region", "fine")
    owner = ("member", "region", "fine")
    fine = P(None, "region", "fine", "member")
    return jax.shard_map(
        shards,
        mesh=mesh,
        in_specs=(
            strip,
            strip,
            strip,
            P("region", "fine"),
            P("region", "fine"),
            P(owner, None, None),
            P(owner, None, None),
            P(owner, None),
            P(owner, None),
            P(owner),
            fine,
        ),
        out_specs=(strip, strip, strip, fine),
        check_vma=False,
    )
```

time: 260 us -> 48.9 us (0.19)
  local copies, waits for them, and re-layouts: 74.7 us -> 2.04 us
  starting transfers between devices: 72.9 us -> 12.2 us
  waiting for transfers between devices: 70.3 us -> 19.7 us
  matrix products: 20.5 us -> 0 us
  other arithmetic: 17.9 us -> 0 us
  Pallas kernels: 0 us -> 13.8 us
    gather x1 -> x0, local copies, waits for them, and re-layouts: 47.1 us -> none  [analyse_regions(): column_block[:, positions]]
    all_to_all x13 -> x2, starting transfers between devices: 48 us -> 11.7 us  [the longest x1 8.19 us: shards(): got = lax.all_to_all(out, owners, split_axis=0, concat_axis=0, tiled=True)]
    all_to_all x13 -> x2, waiting for transfers between devices: 45.5 us -> 18.7 us  [the longest x1 9.37 us: shards(): home = lax.all_to_all(back, owners, split_axis=0, concat_axis=0, tiled=True)]
    ppermute x8 -> x0, starting transfers between devices: 24 us -> none  [shifted(): return lax.ppermute(shard, axis, pairs)]
    dot_general x29 -> x0, matrix products: 20.5 us -> none  [the longest x8 5.42 us: analyse_regions(): jnp.einsum('rij,rjk->rik', factor, inverse_root, precision=HIGHEST)]
    ppermute x8 -> x0, waiting for transfers between devices: 18.6 us -> none  [shifted(): return lax.ppermute(shard, axis, pairs)]
    pallas_call x0 -> x5, Pallas kernels: none -> 13.8 us  [the longest x1 6.04 us: shards(): call(functools.partial(region_kernel, *layout), back_shape, [VMEM] * 3, s...]
    unnamed x48 -> x6, local copies, waits for them, and re-layouts: 15.5 us -> 2.04 us
  transfers between devices with their start and end apart: 29 -> 3, of which waited for: 27 -> 3; matrix products, arithmetic and copies ran while one was open for 9% -> 0% of each run, Pallas kernels for 0% -> 5%
where the time goes in v1:
time: 48.9 us; the launch traced here: 48.4 us
  waiting for transfers between devices  19.7 us (40%)
  Pallas kernels  13.8 us (28%)
  starting transfers between devices  12.2 us (25%)
  local copies, waits for them, and re-layouts  2.04 us (4%)
  between operations  0.66 us (1%)
    all_to_all x1, waiting for transfers between devices, shards(): home = lax.all_to_all(back, owners, split_axis=0, concat_axis=0, tiled=True)  9.37 us
    all_to_all x1, waiting for transfers between devices, shards(): got = lax.all_to_all(out, owners, split_axis=0, concat_axis=0, tiled=True)  9.33 us
    all_to_all x1, starting transfers between devices, shards(): got = lax.all_to_all(out, owners, split_axis=0, concat_axis=0, tiled=True)  8.19 us
    pallas_call x1, Pallas kernels, shards(): call(functools.partial(region_kernel, *layout), back_shape, [VMEM] * 3, s...  6.04 us
    all_to_all x1, starting transfers between devices, shards(): home = lax.all_to_all(back, owners, split_axis=0, concat_axis=0, tiled=True)  3.53 us
    pallas_call x1, Pallas kernels, shards(): call(observe_kernel, (f32(REG_DEV, padded, padded), f32(REG_DEV, padded,...  2.31 us
    unnamed x6, local copies, waits for them, and re-layouts  2.04 us
    pallas_call x1, Pallas kernels, shards(): call(functools.partial(home_kernel, mem, strips, width), (f32(*flat), f32...  1.86 us
  transfers between devices with their start and end apart: 3, of which 3 were waited for; matrix products, arithmetic and copies ran while one was open for 0% of the time, Pallas kernels for 5%

profile of v1, /device:TPU:0, one launch (start us, length us, event | category | flops | bytes accessed | tf_op | source)
XLA Modules:
  0.0 48.4 jit_solution(3977389780091001000)
XLA Ops:
  0.6 1.8 %turn.1 = (f32[264,128]{1,0:T(8,128)}, f32[264,128]{1,0:T(8,128)}, f32[2,8,128]{2,1,0:T(8,128)}) custom-call(f32[128,128]{1,0:T(8,128)} %bitcast.9, f32[128,128]{1,0:T(8,128)} %bitcast.10, f32[128,128]{1,0:T(8,128)} %bitcast.11, f32[1,256]{1,0:T(1,128)} %zonal_ref.1, f32[1,256]{1,0:T(1,128)} %merid_ref.1), custom_call_target="tpu_custom_call" | custom-call | tf_op jit(solution)/shard_map/turn/pallas_call | solution.py:382
  2.4 0.5 %collective-permute-start = (f32[2,8,128]{2,1,0:T(8,128)}, f32[2,8,128]{2,1,0:T(8,128)S(1)}, u32[]{:S(2)}, u32[]{:S(2)}) collective-permute-start(f32[2,8,128]{2,1,0:T(8,128)} %get-tuple-element.15), channel_id=1, source_target_pairs={{1,0},{0,1},{3,2},{2,3},{5,4},{4,5},{7,6},{6,7},{9,8},{8,9},{11,10... | collective-permute-start | bytes 24584 | tf_op jit(solution)/shard_map/ppermute | solution.py:27
  2.9 1.0 %collective-permute-done.west_ref.east_ref = f32[2,8,128]{2,1,0:T(8,128)S(1)} collective-permute-done((f32[2,8,128]{2,1,0:T(8,128)}, f32[2,8,128]{2,1,0:T(8,128)S(1)}, u32[]{:S(2)}, u32[]{:S(2)}) %collective-permute-start) | collective-permute-done | bytes 8224 | tf_op jit(solution)/shard_map/ppermute | solution.py:27
  3.9 0.0 copy-start.2
  3.9 0.6 %copy-done.2 = f32[2,8,128]{2,1,0:T(8,128)} copy-done((f32[2,8,128]{2,1,0:T(8,128)}, f32[2,8,128]{2,1,0:T(8,128)S(1)}, u32[]{:S(2)}) %copy-start.2) | copy-done | bytes 8216
  4.5 1.8 %blocks.1 = f32[16,40,128]{2,1,0:T(8,128)} custom-call(f32[264,128]{1,0:T(8,128)} %get-tuple-element.13.pair_ref, f32[264,128]{1,0:T(8,128)} %get-tuple-element.14.single_ref, f32[2,8,128]{2,1,0:T(8,128)} %copy-done.2, f32[2,8,128]{2,1,0:T(8,128)} %copy-done.2), custom_call_target="tpu_custom_call" | custom-call | tf_op jit(solution)/shard_map/blocks/pallas_call | solution.py:396
  6.3 8.2 %all-to-all-start = ((f32[16,40,128]{2,1,0:T(8,128)}), f32[16,40,128]{2,1,0:T(8,128)S(1)}, u32[]{:S(2)}, u32[]{:S(2)}) async-start(f32[16,40,128]{2,1,0:T(8,128)} %blocks.1), calls=%async_computation | async-start | bytes 655360 | tf_op jit(solution)/shard_map/all_to_all | solution.py:402
  14.5 2.3 %observe.1 = (f32[2,128,128]{2,1,0:T(8,128)}, f32[2,128,128]{2,1,0:T(8,128)}) custom-call(s32[2,4,512]{2,1,0:T(4,128)} %bitcast.15, f32[2,4,512]{2,1,0:T(4,128)} %bitcast.16, f32[2,512]{1,0:T(2,128)} %value_ref.1, f32[2,512]{1,0:T(2,128)} %var_ref.1, s32[2]{0:T(128)} %count_ref.1), custom_call_target="tpu_custom_call" | custom-call | flops 201326592 | bytes 1048576 | tf_op jit(solution)/shard_map/observe/pallas_call | solution.py:409
  16.8 9.3 %all-to-all-done.got_ref = f32[16,40,128]{2,1,0:T(8,128)S(1)} async-done(((f32[16,40,128]{2,1,0:T(8,128)}), f32[16,40,128]{2,1,0:T(8,128)S(1)}, u32[]{:S(2)}, u32[]{:S(2)}) %all-to-all-start) | async-done | bytes 327712 | tf_op jit(solution)/shard_map/all_to_all | solution.py:402
  26.2 0.0 copy-start
  26.2 0.7 %copy-done = f32[16,40,128]{2,1,0:T(8,128)} copy-done((f32[16,40,128]{2,1,0:T(8,128)}, f32[16,40,128]{2,1,0:T(8,128)S(1)}, u32[]{:S(2)}) %copy-start) | copy-done | bytes 327704
  26.9 6.0 %region.1 = f32[16,32,128]{2,1,0:T(8,128)} custom-call(f32[16,40,128]{2,1,0:T(8,128)} %copy-done, f32[2,128,128]{2,1,0:T(8,128)} %get-tuple-element.16.info_ref, f32[2,128,128]{2,1,0:T(8,128)} %get-tuple-element.17.pull_ref), custom_call_target="tpu_custom_call" | custom-call | tf_op jit(solution)/shard_map/region/pallas_call | solution.py:424
  32.9 3.5 %all-to-all-start.1 = ((f32[16,32,128]{2,1,0:T(8,128)}), f32[16,32,128]{2,1,0:T(8,128)S(1)}, u32[]{:S(2)}, u32[]{:S(2)}) async-start(f32[16,32,128]{2,1,0:T(8,128)} %region.1), calls=%async_computation.1 | async-start | bytes 524288 | tf_op jit(solution)/shard_map/all_to_all | solution.py:447
  36.5 9.4 %all-to-all-done.1.got_ref = f32[16,32,128]{2,1,0:T(8,128)S(1)} async-done(((f32[16,32,128]{2,1,0:T(8,128)}), f32[16,32,128]{2,1,0:T(8,128)S(1)}, u32[]{:S(2)}, u32[]{:S(2)}) %all-to-all-start.1) | async-done | bytes 262176 | tf_op jit(solution)/shard_map/all_to_all | solution.py:447
  45.8 0.0 copy-start.1
  45.9 0.7 %copy-done.1 = f32[16,32,128]{2,1,0:T(8,128)} copy-done((f32[16,32,128]{2,1,0:T(8,128)}, f32[16,32,128]{2,1,0:T(8,128)S(1)}, u32[]{:S(2)}) %copy-start.1) | copy-done | bytes 262168
  46.6 1.9 %home.1 = (f32[128,128]{1,0:T(8,128)}, f32[128,128]{1,0:T(8,128)}, f32[128,128]{1,0:T(8,128)}, f32[3,2,1,128]{3,2,1,0:T(1,128)}) custom-call(s32[1]{0:T(128)} %bitcast.group_ref, f32[16,32,128]{2,1,0:T(8,128)} %copy-done.1, f32[3,2,1,128]{3,2,1,0:T(1,128)} %ctrl_ref.1), custom_call_target="tpu_custom_call" | custom-call | tf_op jit(solution)/shard_map/home/pallas_call | solution.py:449
Async XLA Ops:
  2.4 1.5 %collective-permute-start = (f32[2,8,128]{2,1,0:T(8,128)}, f32[2,8,128]{2,1,0:T(8,128)S(1)}, u32[]{:S(2)}, u32[]{:S(2)}) collective-permute-start(f32[2,8,128]{2,1,0:T(8,128)} %get-tuple-element.15), channel_id=1, source_target_pairs={{1,0},{0,1},{3,2},{2,3},{5,4},{4,5},{7,6},{6,7},{9,8},{8,9},{11,10... | collective-permute-start | bytes 24584 | tf_op jit(solution)/shard_map/ppermute | solution.py:27
  3.9 0.6 %copy-start.2 = (f32[2,8,128]{2,1,0:T(8,128)}, f32[2,8,128]{2,1,0:T(8,128)S(1)}, u32[]{:S(2)}) copy-start(f32[2,8,128]{2,1,0:T(8,128)S(1)} %collective-permute-done.west_ref.east_ref) | copy-start | bytes 24580
  6.3 19.8 %all-to-all-start = ((f32[16,40,128]{2,1,0:T(8,128)}), f32[16,40,128]{2,1,0:T(8,128)S(1)}, u32[]{:S(2)}, u32[]{:S(2)}) async-start(f32[16,40,128]{2,1,0:T(8,128)} %blocks.1), calls=%async_computation | async-start | bytes 655360 | tf_op jit(solution)/shard_map/all_to_all | solution.py:402
  26.2 0.7 %copy-start = (f32[16,40,128]{2,1,0:T(8,128)}, f32[16,40,128]{2,1,0:T(8,128)S(1)}, u32[]{:S(2)}) copy-start(f32[16,40,128]{2,1,0:T(8,128)S(1)} %all-to-all-done.got_ref) | copy-start | bytes 983044
  32.9 12.9 %all-to-all-start.1 = ((f32[16,32,128]{2,1,0:T(8,128)}), f32[16,32,128]{2,1,0:T(8,128)S(1)}, u32[]{:S(2)}, u32[]{:S(2)}) async-start(f32[16,32,128]{2,1,0:T(8,128)} %region.1), calls=%async_computation.1 | async-start | bytes 524288 | tf_op jit(solution)/shard_map/all_to_all | solution.py:447
  45.8 0.7 %copy-start.1 = (f32[16,32,128]{2,1,0:T(8,128)}, f32[16,32,128]{2,1,0:T(8,128)S(1)}, u32[]{:S(2)}) copy-start(f32[16,32,128]{2,1,0:T(8,128)S(1)} %all-to-all-done.1.got_ref) | copy-start | bytes 786436

commit v2 on v1

--- a/solution.py
+++ b/solution.py
@@ -13,6 +13,7 @@
 LANES = 128
 TILE = 8
 HALF = LANES // 2
+GRANT = 32 << 20
 
 HIGHEST = lax.Precision.HIGHEST
 NT = (((1,), (1,)), ((), ()))
@@ -341,19 +342,29 @@
 
 
 def call(kernel, out_shape, specs, scratch=(), cost=None, name=None):
+    many = isinstance(out_shape, tuple)
     return pl.pallas_call(
         kernel,
         out_shape=out_shape,
         in_specs=specs,
-        out_specs=jax.tree.map(lambda _: VMEM, out_shape),
+        out_specs=tuple(VMEM for _ in out_shape) if many else VMEM,
         scratch_shapes=scratch,
         cost_estimate=cost,
+        compiler_params=pltpu.CompilerParams(vmem_limit_bytes=GRANT),
         name=name,
     )
 
 
 def f32(*shape):
     return jax.ShapeDtypeStruct(shape, jnp.float32)
+
+
+def near(*shape):
+    return pltpu.VMEM(shape, jnp.float32)
+
+
+def kept(array):
+    return pltpu.with_memory_space_constraint(array, pltpu.VMEM)
 
 
 def shards(
@@ -381,7 +392,7 @@
     flat = (mem * columns // LANES, LANES)
     pair, single, edge = call(
         functools.partial(turn_kernel, mem),
-        (f32(columns + TILE, LANES), f32(columns + TILE, LANES), f32(2, TILE, LANES)),
+        (near(columns + TILE, LANES), near(columns + TILE, LANES), near(2, TILE, LANES)),
         [VMEM] * 5,
         name="turn",
     )(
@@ -395,20 +406,21 @@
     from_east = from_west if lax.axis_size("fine") == 2 else passed_along(edge, "fine", -1)
     out = call(
         functools.partial(blocks_kernel, width),
-        f32(count, OUT_ROWS, LANES),
+        near(count, OUT_ROWS, LANES),
         [VMEM] * 4,
         name="blocks",
-    )(pair, single, from_west, from_east)
+    )(kept(pair), kept(single), kept(from_west), kept(from_east))
     got = lax.all_to_all(out, owners, split_axis=0, concat_axis=0, tiled=True)
+    got = kept(got)
     states = 3 * width * strips // REG_DEV
-    back_shape = f32(count, BACK_ROWS, LANES)
+    back_shape = near(count, BACK_ROWS, LANES)
     layout = (groups, strips, width)
     if states <= members:
         padded = -(-states // LANES) * LANES
         obs = obs_value.shape[1]
         info, pull = call(
             observe_kernel,
-            (f32(REG_DEV, padded, padded), f32(REG_DEV, padded, LANES)),
+            (near(REG_DEV, padded, padded), near(REG_DEV, padded, LANES)),
             [VMEM] * 4 + [SMEM],
             cost=pl.CostEstimate(
                 flops=12 * REG_DEV * padded * padded * obs, bytes_accessed=1 << 20, transcendentals=0
@@ -430,7 +442,7 @@
                 pltpu.VMEM((REG_DEV, padded, members), jnp.float32),
             ],
             name="region",
-        )(got, info, pull)
+        )(got, kept(info), kept(pull))
     else:
         x = call(
             functools.partial(forecast_kernel, *layout),
@@ -451,7 +463,7 @@
         (f32(*flat), f32(*flat), f32(*flat), f32(*fine_ctrl.shape)),
         [SMEM, VMEM, VMEM],
         name="home",
-    )(mine, home, fine_ctrl)
+    )(mine, kept(home), fine_ctrl)
     shape = (mem, rows, columns)
     return (ana_h.reshape(shape), ana_u.reshape(shape), ana_v.reshape(shape), fine_out)
 

time: 48.9 us -> 45.5 us (0.930)
  Pallas kernels: 13.8 us -> 8.2 us
  local copies, waits for them, and re-layouts: 2.04 us -> 3.83 us
    pallas_call x3, Pallas kernels: 5.87 us -> 2.32 us  [the longest x1 1.38 us: shards(): call(observe_kernel, (near(REG_DEV, padded, padded), near(REG_DEV, padded...]
    unnamed x6 -> x22, local copies, waits for them, and re-layouts: 2.04 us -> 3.83 us
    pallas_call x1, Pallas kernels: 6.04 us -> 4.97 us  [shards(): call(functools.partial(region_kernel, *layout), back_shape, [VMEM] * 3, s...]
    pallas_call x1, Pallas kernels: 1.86 us -> 0.91 us  [shards(): call(functools.partial(home_kernel, mem, strips, width), (f32(*flat), f32...]
  transfers between devices with their start and end apart: 3 -> 3, of which waited for: 3 -> 3; matrix products, arithmetic and copies ran while one was open for 0% -> 0% of each run, Pallas kernels for 5% -> 3%
where the time goes in v2:
time: 45.5 us; the launch traced here: 45 us
  waiting for transfers between devices  19.8 us (44%)
  starting transfers between devices  12.4 us (27%)
  Pallas kernels  8.2 us (18%)
  local copies, waits for them, and re-layouts  3.83 us (8%)
  between operations  0.74 us (2%)
    all_to_all x1, waiting for transfers between devices, shards(): got = lax.all_to_all(out, owners, split_axis=0, concat_axis=0, tiled=True)  9.6 us
    all_to_all x1, waiting for transfers between devices, shards(): home = lax.all_to_all(back, owners, split_axis=0, concat_axis=0, tiled=True)  9.36 us
    all_to_all x1, starting transfers between devices, shards(): got = lax.all_to_all(out, owners, split_axis=0, concat_axis=0, tiled=True)  8.34 us
    pallas_call x1, Pallas kernels, shards(): call(functools.partial(region_kernel, *layout), back_shape, [VMEM] * 3, s...  4.97 us
    unnamed x22, local copies, waits for them, and re-layouts  3.83 us
    all_to_all x1, starting transfers between devices, shards(): home = lax.all_to_all(back, owners, split_axis=0, concat_axis=0, tiled=True)  3.53 us
    pallas_call x1, Pallas kernels, shards(): call(observe_kernel, (near(REG_DEV, padded, padded), near(REG_DEV, padded...  1.38 us
  transfers between devices with their start and end apart: 3, of which 3 were waited for; matrix products, arithmetic and copies ran while one was open for 0% of the time, Pallas kernels for 3%

profile of v2, /device:TPU:0, one launch (start us, length us, event | category | flops | bytes accessed | tf_op | source)
XLA Modules:
  0.0 45.0 jit_solution(11829859324935572483)
XLA Ops:
  0.6 0.0 copy-start.5
  0.6 0.0 copy-start.4
  0.7 0.7 %copy-done.5 = f32[1,256]{1,0:T(1,128)S(1)} copy-done((f32[1,256]{1,0:T(1,128)S(1)}, f32[1,256]{1,0:T(1,128)}, u32[]{:S(2)}) %copy-start.5) | copy-done | bytes 1048
  1.3 0.0 copy-done.4
  1.3 0.0 copy-start
  1.3 0.8 %copy-done = f32[64,1,256]{2,1,0:T(1,128)S(1)} copy-done((f32[64,1,256]{2,1,0:T(1,128)S(1)}, f32[64,1,256]{2,1,0:T(1,128)}, u32[]{:S(2)}) %copy-start) | copy-done | bytes 65560
  2.2 0.0 copy-start.1
  2.2 0.8 %copy-done.1 = f32[64,1,256]{2,1,0:T(1,128)S(1)} copy-done((f32[64,1,256]{2,1,0:T(1,128)S(1)}, f32[64,1,256]{2,1,0:T(1,128)}, u32[]{:S(2)}) %copy-start.1) | copy-done | bytes 65560
  3.0 0.0 copy-start.2
  3.0 0.8 %copy-done.2 = f32[64,1,256]{2,1,0:T(1,128)S(1)} copy-done((f32[64,1,256]{2,1,0:T(1,128)S(1)}, f32[64,1,256]{2,1,0:T(1,128)}, u32[]{:S(2)}) %copy-start.2) | copy-done | bytes 65560
  3.8 0.1 turn.1
  4.0 0.6 %collective-permute-start = (f32[2,8,128]{2,1,0:T(8,128)S(1)}, f32[2,8,128]{2,1,0:T(8,128)S(1)}, u32[]{:S(2)}, u32[]{:S(2)}) collective-permute-start(f32[2,8,128]{2,1,0:T(8,128)S(1)} %get-tuple-element.15), channel_id=1, source_target_pairs={{1,0},{0,1},{3,2},{2,3},{5,4},{4,5},{7,6},{6,7},{9,8},{8,9},{11,10... | collective-permute-start | bytes 24584 | tf_op jit(solution)/shard_map/ppermute | solution.py:28
  4.5 0.8 %collective-permute-done.west_ref.east_ref = f32[2,8,128]{2,1,0:T(8,128)S(1)} collective-permute-done((f32[2,8,128]{2,1,0:T(8,128)S(1)}, f32[2,8,128]{2,1,0:T(8,128)S(1)}, u32[]{:S(2)}, u32[]{:S(2)}) %collective-permute-start) | collective-permute-done | bytes 8224 | tf_op jit(solution)/shard_map/ppermute | solution.py:28
  5.4 0.8 %blocks.1 = f32[16,40,128]{2,1,0:T(8,128)} custom-call(f32[264,128]{1,0:T(8,128)S(1)} %get-tuple-element.13.pair_ref, f32[264,128]{1,0:T(8,128)S(1)} %get-tuple-element.14.single_ref, f32[2,8,128]{2,1,0:T(8,128)S(1)} %collective-permute-done.west_ref.east_ref, f32[2,8,128]{2,1,0:T(8,128)S(1)} %collective-permute-done.west_ref.east_ref), custom_call_target="tpu_custom_call" | custom-call | tf_op jit(solution)/shard_map/blocks/pallas_call | solution.py:407
  6.2 0.0 copy-start.6
  6.2 0.0 copy-start.7
  6.2 0.0 copy-start.8
  6.2 8.3 %all-to-all-start = ((f32[16,40,128]{2,1,0:T(8,128)}), f32[16,40,128]{2,1,0:T(8,128)S(1)}, u32[]{:S(2)}, u32[]{:S(2)}) async-start(f32[16,40,128]{2,1,0:T(8,128)} %blocks.1), calls=%async_computation | async-start | bytes 655360 | tf_op jit(solution)/shard_map/all_to_all | solution.py:413
  14.5 0.0 copy-start.10
  14.6 0.0 copy-done.6
  14.6 0.0 copy-done.7
  14.6 0.0 copy-done.8
  14.6 0.0 copy-done.9
  14.6 0.6 %copy-done.10 = s32[2]{0:T(128)S(1)} copy-done((s32[2]{0:T(128)S(1)}, s32[2]{0:T(128)}, u32[]{:S(2)}) %copy-start.10) | copy-done | bytes 32
  15.2 1.4 %observe.1 = (f32[2,128,128]{2,1,0:T(8,128)S(1)}, f32[2,128,128]{2,1,0:T(8,128)S(1)}) custom-call(s32[2,4,512]{2,1,0:T(4,128)S(1)} %bitcast.12, f32[2,4,512]{2,1,0:T(4,128)S(1)} %bitcast.13, f32[2,512]{1,0:T(2,128)S(1)} %copy-done.8, f32[2,512]{1,0:T(2,128)S(1)} %copy-done.9, s32[2]{0:T(128)S(1)} %copy-done.10), custom_call_target="tpu_custom_call" | custom-call | flops 201326592 | bytes 1048576 | tf_op jit(solution)/shard_map/observe/pallas_call | solution.py:421
  16.6 9.6 %all-to-all-done.got_ref = f32[16,40,128]{2,1,0:T(8,128)S(1)} async-done(((f32[16,40,128]{2,1,0:T(8,128)}), f32[16,40,128]{2,1,0:T(8,128)S(1)}, u32[]{:S(2)}, u32[]{:S(2)}) %all-to-all-start) | async-done | bytes 327712 | tf_op jit(solution)/shard_map/all_to_all | solution.py:413
  26.2 5.0 %region.1 = f32[16,32,128]{2,1,0:T(8,128)} custom-call(f32[16,40,128]{2,1,0:T(8,128)S(1)} %all-to-all-done.got_ref, f32[2,128,128]{2,1,0:T(8,128)S(1)} %get-tuple-element.16.info_ref, f32[2,128,128]{2,1,0:T(8,128)S(1)} %get-tuple-element.17.pull_ref), custom_call_target="tpu_custom_call" | custom-call | tf_op jit(solution)/shard_map/region/pallas_call | solution.py:436
  31.2 3.5 %all-to-all-start.1 = ((f32[16,32,128]{2,1,0:T(8,128)}), f32[16,32,128]{2,1,0:T(8,128)S(1)}, u32[]{:S(2)}, u32[]{:S(2)}) async-start(f32[16,32,128]{2,1,0:T(8,128)} %region.1), calls=%async_computation.1 | async-start | bytes 524288 | tf_op jit(solution)/shard_map/all_to_all | solution.py:459
  34.7 0.0 copy-start.3
  34.7 9.4 %all-to-all-done.1.got_ref = f32[16,32,128]{2,1,0:T(8,128)S(1)} async-done(((f32[16,32,128]{2,1,0:T(8,128)}), f32[16,32,128]{2,1,0:T(8,128)S(1)}, u32[]{:S(2)}, u32[]{:S(2)}) %all-to-all-start.1) | async-done | bytes 262176 | tf_op jit(solution)/shard_map/all_to_all | solution.py:459
  44.1 0.0 copy-done.3
  44.1 0.9 %home.1 = (f32[128,128]{1,0:T(8,128)}, f32[128,128]{1,0:T(8,128)}, f32[128,128]{1,0:T(8,128)}, f32[3,2,1,128]{3,2,1,0:T(1,128)}) custom-call(s32[1]{0:T(128)} %bitcast.group_ref, f32[16,32,128]{2,1,0:T(8,128)S(1)} %all-to-all-done.1.got_ref, f32[3,2,1,128]{3,2,1,0:T(1,128)S(1)} %copy-done.3), custom_call_target="tpu_custom_call" | custom-call | tf_op jit(solution)/shard_map/home/pallas_call | solution.py:461
  (1 shorter events, 0.0 us)
Async XLA Ops:
  0.6 0.7 %copy-start.5 = (f32[1,256]{1,0:T(1,128)S(1)}, f32[1,256]{1,0:T(1,128)}, u32[]{:S(2)}) copy-start(f32[1,256]{1,0:T(1,128)} %merid_ref.1) | copy-start | bytes 3076
  0.6 0.7 %copy-start.4 = (f32[1,256]{1,0:T(1,128)S(1)}, f32[1,256]{1,0:T(1,128)}, u32[]{:S(2)}) copy-start(f32[1,256]{1,0:T(1,128)} %zonal_ref.1) | copy-start | bytes 3076
  1.3 0.8 %copy-start = (f32[64,1,256]{2,1,0:T(1,128)S(1)}, f32[64,1,256]{2,1,0:T(1,128)}, u32[]{:S(2)}) copy-start(f32[64,1,256]{2,1,0:T(1,128)} %param.11) | copy-start | bytes 196612
  2.2 0.8 %copy-start.1 = (f32[64,1,256]{2,1,0:T(1,128)S(1)}, f32[64,1,256]{2,1,0:T(1,128)}, u32[]{:S(2)}) copy-start(f32[64,1,256]{2,1,0:T(1,128)} %param.12) | copy-start | bytes 196612
  3.0 0.8 %copy-start.2 = (f32[64,1,256]{2,1,0:T(1,128)S(1)}, f32[64,1,256]{2,1,0:T(1,128)}, u32[]{:S(2)}) copy-start(f32[64,1,256]{2,1,0:T(1,128)} %param.13) | copy-start | bytes 196612
  4.0 1.4 %collective-permute-start = (f32[2,8,128]{2,1,0:T(8,128)S(1)}, f32[2,8,128]{2,1,0:T(8,128)S(1)}, u32[]{:S(2)}, u32[]{:S(2)}) collective-permute-start(f32[2,8,128]{2,1,0:T(8,128)S(1)} %get-tuple-element.15), channel_id=1, source_target_pairs={{1,0},{0,1},{3,2},{2,3},{5,4},{4,5},{7,6},{6,7},{9,8},{8,9},{11,10... | collective-permute-start | bytes 24584 | tf_op jit(solution)/shard_map/ppermute | solution.py:28
  6.2 8.4 %copy-start.6 = (s32[2,512,4]{1,2,0:T(4,128)S(1)}, s32[2,512,4]{1,2,0:T(4,128)}, u32[]{:S(2)}) copy-start(s32[2,512,4]{1,2,0:T(4,128)} %param.16) | copy-start | bytes 49156
  6.2 8.4 %copy-start.7 = (f32[2,512,4]{1,2,0:T(4,128)S(1)}, f32[2,512,4]{1,2,0:T(4,128)}, u32[]{:S(2)}) copy-start(f32[2,512,4]{1,2,0:T(4,128)} %param.17) | copy-start | bytes 49156
  6.2 8.4 %copy-start.8 = (f32[2,512]{1,0:T(2,128)S(1)}, f32[2,512]{1,0:T(2,128)}, u32[]{:S(2)}) copy-start(f32[2,512]{1,0:T(2,128)} %value_ref.1) | copy-start | bytes 12292
  6.2 8.4 %copy-start.9 = (f32[2,512]{1,0:T(2,128)S(1)}, f32[2,512]{1,0:T(2,128)}, u32[]{:S(2)}) copy-start(f32[2,512]{1,0:T(2,128)} %var_ref.1) | copy-start | bytes 12292
  6.2 20.0 %all-to-all-start = ((f32[16,40,128]{2,1,0:T(8,128)}), f32[16,40,128]{2,1,0:T(8,128)S(1)}, u32[]{:S(2)}, u32[]{:S(2)}) async-start(f32[16,40,128]{2,1,0:T(8,128)} %blocks.1), calls=%async_computation | async-start | bytes 655360 | tf_op jit(solution)/shard_map/all_to_all | solution.py:413
  14.5 0.7 %copy-start.10 = (s32[2]{0:T(128)S(1)}, s32[2]{0:T(128)}, u32[]{:S(2)}) copy-start(s32[2]{0:T(128)} %count_ref.1) | copy-start | bytes 28
  31.2 12.9 %all-to-all-start.1 = ((f32[16,32,128]{2,1,0:T(8,128)}), f32[16,32,128]{2,1,0:T(8,128)S(1)}, u32[]{:S(2)}, u32[]{:S(2)}) async-start(f32[16,32,128]{2,1,0:T(8,128)} %region.1), calls=%async_computation.1 | async-start | bytes 524288 | tf_op jit(solution)/shard_map/all_to_all | solution.py:459
  34.7 9.4 %copy-start.3 = (f32[3,2,1,128]{3,2,1,0:T(1,128)S(1)}, f32[3,2,1,128]{3,2,1,0:T(1,128)}, u32[]{:S(2)}) copy-start(f32[3,2,1,128]{3,2,1,0:T(1,128)} %ctrl_ref.1) | copy-start | bytes 9220

commit v3 on v2

--- a/solution.py
+++ b/solution.py
@@ -20,6 +20,7 @@
 NN = (((1,), (0,)), ((), ()))
 VMEM = pl.BlockSpec(memory_space=pltpu.VMEM)
 SMEM = pl.BlockSpec(memory_space=pltpu.SMEM)
+HBM = pl.BlockSpec(memory_space=pltpu.HBM)
 
 
 def passed_along(block, axis, distance):
@@ -66,7 +67,17 @@
 BACK_ROWS = 4 * TILE
 
 
-def turn_kernel(mem, h_ref, u_ref, v_ref, zonal_ref, merid_ref, pair_ref, single_ref, edge_ref):
+def turn_kernel(mem, later, *refs):
+    h_ref, u_ref, v_ref, zonal_ref, merid_ref, count_ref = refs[:6]
+    sources, refs = refs[6 : 6 + later], refs[6 + later :]
+    pair_ref, single_ref, edge_ref, live_ref = refs[:4]
+    targets, sems = refs[4 : 4 + later], refs[-1]
+    copies = [
+        pltpu.make_async_copy(source, target, sems.at[i])
+        for i, (source, target) in enumerate(zip(sources, targets))
+    ]
+    for copy in copies:
+        copy.start()
     tiles = h_ref.shape[0] // mem
     columns = tiles * LANES
     zero = jnp.zeros((TILE, LANES), jnp.float32)
@@ -86,9 +97,14 @@
     early = row_of((TILE, LANES)) < STEPS
     for i, ref in enumerate((pair_ref, single_ref)):
         edge_ref[i] = jnp.where(early, ref[columns : columns + TILE, :], ref[0:TILE, :])
-
-
-def blocks_kernel(width, pair_ref, single_ref, west_ref, east_ref, send_ref):
+    for q in range(REG_DEV):
+        live_ref[q] = jnp.full(live_ref.shape[1:], count_ref[q], jnp.int32)
+    for copy in copies:
+        copy.wait()
+
+
+def blocks_kernel(width, pair_ref, single_ref, west_ref, east_ref, *refs):
+    send_ref = refs[-1]
     count = send_ref.shape[0]
     shape = (TILE, LANES)
     early = row_of(shape) < STEPS
@@ -169,7 +185,7 @@
                 x_ref[q, place, lanes] = pltpu.roll(field[r], span - STEPS, 0)[:width]
 
 
-def observe_kernel(index_ref, weight_ref, value_ref, var_ref, count_ref, info_ref, pull_ref):
+def observe_kernel(live_ref, index_ref, weight_ref, value_ref, var_ref, info_ref, pull_ref):
     states = info_ref.shape[1]
     obs = index_ref.shape[2]
     for q in range(REG_DEV):
@@ -178,7 +194,7 @@
         for j in range(index_ref.shape[1]):
             hit = state == index_ref[q, j : j + 1, :]
             operator = operator + jnp.where(hit, weight_ref[q, j : j + 1, :], 0.0)
-        live = lane_of((1, obs)) < count_ref[q]
+        live = lane_of((1, obs)) < live_ref[q, 0:1, 0:1]
         inverse = jnp.where(live, 1.0 / var_ref[q : q + 1, :], 0.0)
         scaled = operator * inverse
         info_ref[q] = lax.dot_general(
@@ -268,7 +284,7 @@
     pack(groups, strips, width, ana_ref, increments, send_ref)
 
 
-def home_kernel(mem, strips, width, group_ref, got_ref, ctrl_ref, h_ref, u_ref, v_ref, fine_ref):
+def home_kernel(mem, strips, width, got_ref, ctrl_ref, h_ref, u_ref, v_ref, fine_ref):
     blocks = got_ref.shape[0]
     tiles = blocks * width // LANES
     per_tile = LANES // width
@@ -282,7 +298,7 @@
             turned = jnp.concatenate(rows, axis=0).T
             out_ref[pl.ds(t, mem, stride=tiles), :] = turned[:mem]
             out_ref[pl.ds(t + 1, mem, stride=tiles), :] = turned[mem:]
-    mine = group_ref[0] * strips
+    mine = lax.axis_index("member") * strips
     per_fine = LANES // (2 * width)
     row = row_of((width, LANES))
     lane = lane_of((width, LANES))
@@ -363,6 +379,10 @@
     return pltpu.VMEM(shape, jnp.float32)
 
 
+def far(array):
+    return pltpu.with_memory_space_constraint(array, pltpu.HBM)
+
+
 def kept(array):
     return pltpu.with_memory_space_constraint(array, pltpu.VMEM)
 
@@ -390,49 +410,58 @@
     assert rows == 1 and 2 * mem == LANES and width == 2 * TILE and STEPS * 2 == TILE
     assert columns % (2 * LANES) == 0 and groups % 2 == 0 and strips % REG_DEV == 0
     flat = (mem * columns // LANES, LANES)
-    pair, single, edge = call(
-        functools.partial(turn_kernel, mem),
-        (near(columns + TILE, LANES), near(columns + TILE, LANES), near(2, TILE, LANES)),
-        [VMEM] * 5,
+    states = 3 * width * strips // REG_DEV
+    small = states <= members
+    later = [fine_ctrl]
+    if small:
+        later += [obs_index.transpose(0, 2, 1), obs_weight.transpose(0, 2, 1), obs_value, obs_var]
+    pair, single, edge, live, ctrl, *seen = call(
+        functools.partial(turn_kernel, mem, len(later)),
+        (
+            near(columns + TILE, LANES),
+            near(columns + TILE, LANES),
+            near(2, TILE, LANES),
+            pltpu.VMEM((REG_DEV, TILE, LANES), jnp.int32),
+            *(pltpu.VMEM(array.shape, array.dtype) for array in later),
+        ),
+        [VMEM] * 5 + [SMEM] + [HBM] * len(later),
+        scratch=[pltpu.SemaphoreType.DMA((len(later),))],
         name="turn",
     )(
-        sample_surface_elevation.reshape(flat),
-        sample_zonal_current.reshape(flat),
-        sample_meridional_current.reshape(flat),
-        zonal_edge_layer_courant,
-        meridional_edge_layer_courant,
+        far(sample_surface_elevation.reshape(flat)),
+        far(sample_zonal_current.reshape(flat)),
+        far(sample_meridional_current.reshape(flat)),
+        far(zonal_edge_layer_courant),
+        far(meridional_edge_layer_courant),
+        far(obs_count),
+        *(far(array) for array in later),
     )
     from_west = passed_along(edge, "fine", 1)
     from_east = from_west if lax.axis_size("fine") == 2 else passed_along(edge, "fine", -1)
-    out = call(
-        functools.partial(blocks_kernel, width),
-        near(count, OUT_ROWS, LANES),
-        [VMEM] * 4,
-        name="blocks",
-    )(kept(pair), kept(single), kept(from_west), kept(from_east))
-    got = lax.all_to_all(out, owners, split_axis=0, concat_axis=0, tiled=True)
-    got = kept(got)
-    states = 3 * width * strips // REG_DEV
-    back_shape = near(count, BACK_ROWS, LANES)
-    layout = (groups, strips, width)
-    if states <= members:
+    beside = []
+    if small:
         padded = -(-states // LANES) * LANES
         obs = obs_value.shape[1]
         info, pull = call(
             observe_kernel,
             (near(REG_DEV, padded, padded), near(REG_DEV, padded, LANES)),
-            [VMEM] * 4 + [SMEM],
+            [VMEM] * 5,
             cost=pl.CostEstimate(
                 flops=12 * REG_DEV * padded * padded * obs, bytes_accessed=1 << 20, transcendentals=0
             ),
             name="observe",
-        )(
-            obs_index.transpose(0, 2, 1),
-            obs_weight.transpose(0, 2, 1),
-            obs_value,
-            obs_var,
-            obs_count,
-        )
+        )(kept(live), *(kept(array) for array in seen))
+        beside = [kept(pull)]
+    out = call(
+        functools.partial(blocks_kernel, width),
+        near(count, OUT_ROWS, LANES),
+        [VMEM] * (4 + len(beside)),
+        name="blocks",
+    )(kept(pair), kept(single), kept(from_west), kept(from_east), *beside)
+    got = kept(lax.all_to_all(out, owners, split_axis=0, concat_axis=0, tiled=True))
+    back_shape = near(count, BACK_ROWS, LANES)
+    layout = (groups, strips, width)
+    if small:
         back = call(
             functools.partial(region_kernel, *layout),
             back_shape,
@@ -457,13 +486,12 @@
             functools.partial(pack_kernel, *layout), back_shape, [VMEM] * 2, name="pack"
         )(analysis, increment)
     home = lax.all_to_all(back, owners, split_axis=0, concat_axis=0, tiled=True)
-    mine = lax.axis_index("member").astype(jnp.int32).reshape(1)
     ana_h, ana_u, ana_v, fine_out = call(
         functools.partial(home_kernel, mem, strips, width),
         (f32(*flat), f32(*flat), f32(*flat), f32(*fine_ctrl.shape)),
-        [SMEM, VMEM, VMEM],
+        [VMEM, VMEM],
         name="home",
-    )(mine, kept(home), fine_ctrl)
+    )(kept(home), kept(ctrl))
     shape = (mem, rows, columns)
     return (ana_h.reshape(shape), ana_u.reshape(shape), ana_v.reshape(shape), fine_out)
 

time: 45.5 us -> 41.8 us (0.919)
  blocking collectives: 0 us -> 32.3 us
  waiting for transfers between devices: 19.8 us -> 0.01 us
  starting transfers between devices: 12.4 us -> 0.56 us
  local copies, waits for them, and re-layouts: 3.83 us -> 0 us
    all_to_all x0 -> x2, blocking collectives: none -> 32.3 us  [the longest x1 19.6 us: shards(): lax.all_to_all(out, owners, split_axis=0, concat_axis=0, tiled=True)]
    all_to_all x2 -> x0, waiting for transfers between devices: 19 us -> none  [the longest x1 9.6 us: shards(): got = lax.all_to_all(out, owners, split_axis=0, concat_axis=0, tiled=True)]
    all_to_all x2 -> x0, starting transfers between devices: 11.9 us -> none  [the longest x1 8.34 us: shards(): got = lax.all_to_all(out, owners, split_axis=0, concat_axis=0, tiled=True)]
    unnamed x22 -> x0, local copies, waits for them, and re-layouts: 3.83 us -> none
    pallas_call x1, Pallas kernels: 0.14 us -> 1.75 us  [shards(): call(functools.partial(turn_kernel, mem, len(later)), (near(columns + TIL...]
    ppermute x1, waiting for transfers between devices: 0.83 us -> 0.01 us  [passed_along(): return lax.ppermute(block, axis, route)]
    pallas_call x1, Pallas kernels: 0.81 us -> 0.09 us  [shards(): call(functools.partial(blocks_kernel, width), near(count, OUT_ROWS, LANES...]
    pallas_call x1, Pallas kernels: 4.97 us -> 4.26 us  [shards(): call(functools.partial(region_kernel, *layout), back_shape, [VMEM] * 3, s...]
  transfers between devices with their start and end apart: 3 -> 1, of which waited for: 3 -> 0; matrix products, arithmetic and copies ran while one was open for 0% -> 0% of each run, Pallas kernels for 3% -> 2%
where the time goes in v3:
time: 41.8 us; the launch traced here: 41.5 us
  blocking collectives  32.3 us (77%)
  Pallas kernels  7.9 us (19%)
  between operations  0.67 us (2%)
  starting transfers between devices  0.56 us (1%)
    all_to_all x1, blocking collectives, shards(): lax.all_to_all(out, owners, split_axis=0, concat_axis=0, tiled=True)  19.6 us
    all_to_all x1, blocking collectives, shards(): home = lax.all_to_all(back, owners, split_axis=0, concat_axis=0, tiled=True)  12.7 us
    pallas_call x1, Pallas kernels, shards(): call(functools.partial(region_kernel, *layout), back_shape, [VMEM] * 3, s...  4.26 us
    pallas_call x1, Pallas kernels, shards(): call(functools.partial(turn_kernel, mem, len(later)), (near(columns + TIL...  1.75 us
    pallas_call x1, Pallas kernels, shards(): call(functools.partial(home_kernel, mem, strips, width), (f32(*flat), f32...  0.91 us
    pallas_call x1, Pallas kernels, shards(): call(observe_kernel, (near(REG_DEV, padded, padded), near(REG_DEV, padded...  0.89 us
  transfers between devices with their start and end apart: 1, of which 0 were waited for; matrix products, arithmetic and copies ran while one was open for 0% of the time, Pallas kernels for 2%

profile of v3, /device:TPU:0, one launch (start us, length us, event | category | flops | bytes accessed | tf_op | source)
XLA Modules:
  0.0 41.5 jit_solution(15493300272589606529)
XLA Ops:
  0.6 1.7 %turn.1 = (f32[264,128]{1,0:T(8,128)S(1)}, f32[264,128]{1,0:T(8,128)S(1)}, f32[2,8,128]{2,1,0:T(8,128)S(1)}, s32[2,8,128]{2,1,0:T(8,128)S(1)}, f32[3,2,1,128]{3,...) custom-call(f32[128,128]{1,0:T(8,128)} %bitcast.8, ...), custom_call_target="tpu_custom_call" | custom-call | tf_op jit(solution)/shard_map/turn/pallas_call | solution.py:418
  2.4 0.6 %collective-permute-start = (f32[2,8,128]{2,1,0:T(8,128)S(1)}, f32[2,8,128]{2,1,0:T(8,128)S(1)}, u32[]{:S(2)}, u32[]{:S(2)}) collective-permute-start(f32[2,8,128]{2,1,0:T(8,128)S(1)} %get-tuple-element.21), channel_id=1, source_target_pairs={{1,0},{0,1},{3,2},{2,3},{5,4},{4,5},{7,6},{6,7},{9,8},{8,9},{11,10... | collective-permute-start | bytes 24584 | tf_op jit(solution)/shard_map/ppermute | solution.py:29
  2.9 0.9 %observe.1 = (f32[2,128,128]{2,1,0:T(8,128)S(1)}, f32[2,128,128]{2,1,0:T(8,128)S(1)}) custom-call(s32[2,8,128]{2,1,0:T(8,128)S(1)} %get-tuple-element.22.live_ref, s32[2,4,512]{2,1,0:T(4,128)S(1)} %get-tuple-element.23.index_ref, f32[2,4,512]{2,1,0:T(4,128)S(1)} %get-tuple-element.24.weight_ref, f32[2,512]{1,0:T(2,128)S(1)} %get-tuple-element.25.value_ref, ...), custom_call_target="tpu_custom_call" | custom-call | flops 201326592 | bytes 1048576 | tf_op jit(solution)/shard_map/observe/pallas_call | solution.py:445
  3.8 0.0 collective-permute-done.west_ref.east_ref
  3.9 0.1 blocks.1
  3.9 19.6 %all_to_all.10.got_ref = f32[16,40,128]{2,1,0:T(8,128)S(1)} all-to-all(f32[16,40,128]{2,1,0:T(8,128)S(1)} %blocks.1), channel_id=1, replica_groups=mesh['member'=4,'region'=4,'fine'=2] {'member','region'}, dimensions={0} | all-to-all | bytes 655360 | tf_op jit(solution)/shard_map/all_to_all | solution.py:461
  23.6 4.3 %region.1 = f32[16,32,128]{2,1,0:T(8,128)S(1)} custom-call(f32[16,40,128]{2,1,0:T(8,128)S(1)} %all_to_all.10.got_ref, f32[2,128,128]{2,1,0:T(8,128)S(1)} %get-tuple-element.28.info_ref, f32[2,128,128]{2,1,0:T(8,128)S(1)} %get-tuple-element.27.refs_0_.pull_ref), custom_call_target="tpu_custom_call" | custom-call | tf_op jit(solution)/shard_map/region/pallas_call | solution.py:465
  27.9 12.7 %all_to_all.11.got_ref = f32[16,32,128]{2,1,0:T(8,128)S(1)} all-to-all(f32[16,32,128]{2,1,0:T(8,128)S(1)} %region.1), channel_id=1, replica_groups=mesh['member'=4,'region'=4,'fine'=2] {'member','region'}, dimensions={0} | all-to-all | bytes 524288 | tf_op jit(solution)/shard_map/all_to_all | solution.py:488
  40.6 0.9 %home.1 = (f32[128,128]{1,0:T(8,128)}, f32[128,128]{1,0:T(8,128)}, f32[128,128]{1,0:T(8,128)}, f32[3,2,1,128]{3,2,1,0:T(1,128)}) custom-call(f32[16,32,128]{2,1,0:T(8,128)S(1)} %all_to_all.11.got_ref, f32[3,2,1,128]{3,2,1,0:T(1,128)S(1)} %get-tuple-element.29.ctrl_ref), custom_call_target="tpu_custom_call" | custom-call | tf_op jit(solution)/shard_map/home/pallas_call | solution.py:489
Async XLA Ops:
  2.4 1.5 %collective-permute-start = (f32[2,8,128]{2,1,0:T(8,128)S(1)}, f32[2,8,128]{2,1,0:T(8,128)S(1)}, u32[]{:S(2)}, u32[]{:S(2)}) collective-permute-start(f32[2,8,128]{2,1,0:T(8,128)S(1)} %get-tuple-element.21), channel_id=1, source_target_pairs={{1,0},{0,1},{3,2},{2,3},{5,4},{4,5},{7,6},{6,7},{9,8},{8,9},{11,10... | collective-permute-start | bytes 24584 | tf_op jit(solution)/shard_map/ppermute | solution.py:29

commit v4 on v3

--- a/solution.py
+++ b/solution.py
@@ -54,13 +54,27 @@
     return high, (value - high.astype(jnp.float32)).astype(jnp.bfloat16)
 
 
-def product(left, right, dims=NN):
-    left_high, left_low = split(left)
-    right_high, right_low = split(right)
-    dot = functools.partial(
-        lax.dot_general, dimension_numbers=dims, preferred_element_type=jnp.float32
-    )
-    return dot(left_high, right_high) + (dot(left_high, right_low) + dot(left_low, right_high))
+def beside(value):
+    return jnp.concatenate(split(value), axis=1)
+
+
+def stacked(value):
+    both = jnp.concatenate(split(value), axis=1)
+    return jnp.concatenate([both, both], axis=0)
+
+
+def times(left, right):
+    out = lax.dot_general(left, right, NN, preferred_element_type=jnp.float32)
+    half = out.shape[1] // 2
+    return out[:, :half] + out[:, half:]
+
+
+def squared(value):
+    both = jnp.concatenate(split(value), axis=0)
+    out = lax.dot_general(both, both, NT, preferred_element_type=jnp.float32)
+    half = out.shape[0] // 2
+    out = out[:, :half] + out[:, half:]
+    return out[:half] + out[half:]
 
 
 OUT_ROWS = 5 * TILE
@@ -68,22 +82,24 @@
 
 
 def turn_kernel(mem, later, *refs):
-    h_ref, u_ref, v_ref, zonal_ref, merid_ref, count_ref = refs[:6]
-    sources, refs = refs[6 : 6 + later], refs[6 + later :]
+    sources, refs = refs[: 6 + later], refs[6 + later :]
     pair_ref, single_ref, edge_ref, live_ref = refs[:4]
-    targets, sems = refs[4 : 4 + later], refs[-1]
+    targets, sems = refs[4 + later : -1] + refs[4 : 4 + later], refs[-1]
     copies = [
         pltpu.make_async_copy(source, target, sems.at[i])
         for i, (source, target) in enumerate(zip(sources, targets))
     ]
     for copy in copies:
         copy.start()
+    h_ref, u_ref, v_ref, zonal_ref, merid_ref, count_ref = targets[:6]
     tiles = h_ref.shape[0] // mem
     columns = tiles * LANES
     zero = jnp.zeros((TILE, LANES), jnp.float32)
     for ref in (pair_ref, single_ref):
         ref[0:TILE, :] = zero
         ref[columns : columns + TILE, :] = zero
+    for copy in copies[:5]:
+        copy.wait()
     for t in range(tiles):
         rows = pl.ds(t, mem, stride=tiles)
         lanes = slice(t * LANES, (t + 1) * LANES)
@@ -97,10 +113,10 @@
     early = row_of((TILE, LANES)) < STEPS
     for i, ref in enumerate((pair_ref, single_ref)):
         edge_ref[i] = jnp.where(early, ref[columns : columns + TILE, :], ref[0:TILE, :])
+    for copy in copies[5:]:
+        copy.wait()
     for q in range(REG_DEV):
         live_ref[q] = jnp.full(live_ref.shape[1:], count_ref[q], jnp.int32)
-    for copy in copies:
-        copy.wait()
 
 
 def blocks_kernel(width, pair_ref, single_ref, west_ref, east_ref, *refs):
@@ -211,40 +227,69 @@
     identity = jnp.where(diagonal, 1.0, 0.0)
     regions = range(REG_DEV)
     scale = 1.0 / (members - 1)
-    means, spreads, covs, inverses, iterates, norms = [], [], [], [], [], []
+
+    def as_row(column):
+        return jnp.sum(jnp.where(diagonal, column, 0.0), axis=0, keepdims=True)
+
+    def applied(matrix, row):
+        return jnp.sum(matrix * row, axis=1, keepdims=True)
+
+    x = [x_ref[q] for q in regions]
+    means = [jnp.sum(x[q], axis=1, keepdims=True) / members for q in regions]
+    spreads = [x[q] - means[q] for q in regions]
+    covs = [squared(spreads[q]) for q in regions]
+    gains = [times(beside(covs[q]), stacked(info_ref[q] * scale)) for q in regions]
+    rights = [stacked(gains[q]) for q in regions]
+    gains_2 = [times(beside(gains[q]), rights[q]) for q in regions]
+    pulls, inverse_norms, firsts, iterates, inverses = [], [], [], [], []
     for q in regions:
-        x = x_ref[q]
-        mean = jnp.sum(x, axis=1, keepdims=True) / members
-        spread = x - mean
-        means.append(mean)
-        spreads.append(spread)
-        covs.append(product(spread, spread, NT))
+        pulled = pull_ref[q][:, 0:1] - applied(info_ref[q], as_row(means[q]))
+        pulls.append(jnp.sum(covs[q] * pulled, axis=0, keepdims=True))
+        trace = jnp.sum(jnp.where(diagonal, gains_2[q] + 2.0 * gains[q], 0.0), keepdims=True)
+        inverse_norms.append(lax.rsqrt(trace + members))
     for q in regions:
-        info = info_ref[q]
-        gain = product(covs[q], info) * scale
-        gain_t = product(info, covs[q]) * scale
-        total = jnp.sum(gain * gain_t + jnp.where(diagonal, 2.0 * gain, 0.0), keepdims=True)
-        frobenius = jnp.sqrt(total + members)
-        norms.append(frobenius)
-        iterates.append((identity + gain) / frobenius)
-    factors = [1.5 * identity - 0.5 * iterates[q] for q in regions]
-    iterates = [product(iterates[q], factors[q]) for q in regions]
-    inverses = factors
-    for sweep in range(1, NEWTON):
-        factors = [1.5 * identity - 0.5 * product(inverses[q], iterates[q]) for q in regions]
-        if sweep < NEWTON - 1:
-            iterates = [product(iterates[q], factors[q]) for q in regions]
-        inverses = [product(factors[q], inverses[q]) for q in regions]
+        norm = inverse_norms[q]
+        first = (identity + gains[q]) * norm
+        second = (identity + 2.0 * gains[q] + gains_2[q]) * (norm * norm)
+        third = (second + times(beside(second), rights[q])) * norm
+        inverses.append(1.5 * identity - 0.5 * first)
+        iterates.append(2.25 * first - 1.5 * second + 0.25 * third)
+    for sweep in range(1, NEWTON - 1):
+        rights = [stacked(iterates[q]) for q in regions]
+        lefts = [
+            jnp.concatenate([beside(iterates[q]), beside(inverses[q])], axis=0) for q in regions
+        ]
+        both = [times(lefts[q], rights[q]) for q in regions]
+        seconds = [both[q][:states] for q in regions]
+        thirds = [times(beside(seconds[q]), rights[q]) for q in regions]
+        inverses = [1.5 * inverses[q] - 0.5 * both[q][states:] for q in regions]
+        iterates = [
+            2.25 * iterates[q] - 1.5 * seconds[q] + 0.25 * thirds[q] for q in regions
+        ]
     increments = []
     for q in regions:
-        root = inverses[q] / jnp.sqrt(norms[q])
-        mean_row = jnp.sum(jnp.where(diagonal, means[q], 0.0), axis=0, keepdims=True)
-        pulled = pull_ref[q][:, 0:1] - jnp.sum(info_ref[q] * mean_row, axis=1, keepdims=True)
-        pulled = jnp.sum(covs[q] * pulled, axis=0, keepdims=True)
-        shift = jnp.sum(root * pulled, axis=1, keepdims=True) * scale
-        out_ref[q] = product(root, spreads[q] + shift) + means[q]
-        shift_row = jnp.sum(jnp.where(diagonal, shift, 0.0), axis=0, keepdims=True)
-        increments.append(jnp.sum(root * shift_row, axis=1, keepdims=True))
+        high, low = split(spreads[q])
+        wide = beside(inverses[q])
+        moved = lax.dot_general(
+            wide, jnp.concatenate([high, high], axis=0), NN, preferred_element_type=jnp.float32
+        )
+        moved = moved + lax.dot_general(
+            wide[:, :states], low, NN, preferred_element_type=jnp.float32
+        )
+        twice = applied(inverses[q], as_row(applied(inverses[q], pulls[q])))
+        factor = 1.5 * identity - 0.5 * iterates[q]
+        twice = applied(factor, as_row(applied(factor, as_row(twice))))
+        increment = twice * (inverse_norms[q] * scale)
+        increments.append(increment)
+        high, low = split(moved * jnp.sqrt(inverse_norms[q]))
+        wide = beside(factor)
+        moved = lax.dot_general(
+            wide, jnp.concatenate([high, high], axis=0), NN, preferred_element_type=jnp.float32
+        )
+        moved = moved + lax.dot_general(
+            wide[:, :states], low, NN, preferred_element_type=jnp.float32
+        )
+        out_ref[q] = moved + (means[q] + increment)
     return increments
 
 
@@ -424,8 +469,13 @@
             pltpu.VMEM((REG_DEV, TILE, LANES), jnp.int32),
             *(pltpu.VMEM(array.shape, array.dtype) for array in later),
         ),
-        [VMEM] * 5 + [SMEM] + [HBM] * len(later),
-        scratch=[pltpu.SemaphoreType.DMA((len(later),))],
+        [HBM] * (6 + len(later)),
+        scratch=[
+            *[pltpu.VMEM(flat, jnp.float32)] * 3,
+            *[pltpu.VMEM((1, columns), jnp.float32)] * 2,
+            pltpu.SMEM((REG_DEV,), jnp.int32),
+            pltpu.SemaphoreType.DMA((6 + len(later),)),
+        ],
         name="turn",
     )(
         far(sample_surface_elevation.reshape(flat)),
@@ -438,7 +488,7 @@
     )
     from_west = passed_along(edge, "fine", 1)
     from_east = from_west if lax.axis_size("fine") == 2 else passed_along(edge, "fine", -1)
-    beside = []
+    ahead = []
     if small:
         padded = -(-states // LANES) * LANES
         obs = obs_value.shape[1]
@@ -451,13 +501,13 @@
             ),
             name="observe",
         )(kept(live), *(kept(array) for array in seen))
-        beside = [kept(pull)]
+        ahead = [kept(pull)]
     out = call(
         functools.partial(blocks_kernel, width),
         near(count, OUT_ROWS, LANES),
-        [VMEM] * (4 + len(beside)),
+        [VMEM] * (4 + len(ahead)),
         name="blocks",
-    )(kept(pair), kept(single), kept(from_west), kept(from_east), *beside)
+    )(kept(pair), kept(single), kept(from_west), kept(from_east), *ahead)
     got = kept(lax.all_to_all(out, owners, split_axis=0, concat_axis=0, tiled=True))
     back_shape = near(count, BACK_ROWS, LANES)
     layout = (groups, strips, width)

time: 41.8 us -> 40.4 us (0.967)
  Pallas kernels: 7.9 us -> 6.58 us
    pallas_call x1, Pallas kernels: 4.26 us -> 3.52 us  [shards(): call(functools.partial(region_kernel, *layout), back_shape, [VMEM] * 3, s...]
    pallas_call x1, Pallas kernels: 1.75 us -> 1.17 us  [shards(): call(functools.partial(turn_kernel, mem, len(later)), (near(columns + TIL...]
where the time goes in v4:
time: 40.4 us; the launch traced here: 40.2 us
  blocking collectives  32.3 us (80%)
  Pallas kernels  6.58 us (16%)
  between operations  0.67 us (2%)
  starting transfers between devices  0.56 us (1%)
    all_to_all x1, blocking collectives, shards(): lax.all_to_all(out, owners, split_axis=0, concat_axis=0, tiled=True)  19.6 us
    all_to_all x1, blocking collectives, shards(): home = lax.all_to_all(back, owners, split_axis=0, concat_axis=0, tiled=True)  12.7 us
    pallas_call x1, Pallas kernels, shards(): call(functools.partial(region_kernel, *layout), back_shape, [VMEM] * 3, s...  3.52 us
    pallas_call x1, Pallas kernels, shards(): call(functools.partial(turn_kernel, mem, len(later)), (near(columns + TIL...  1.17 us
    pallas_call x1, Pallas kernels, shards(): call(functools.partial(home_kernel, mem, strips, width), (f32(*flat), f32...  0.91 us
    pallas_call x1, Pallas kernels, shards(): call(observe_kernel, (near(REG_DEV, padded, padded), near(REG_DEV, padded...  0.89 us
  transfers between devices with their start and end apart: 1, of which 0 were waited for; matrix products, arithmetic and copies ran while one was open for 0% of the time, Pallas kernels for 2%

profile of v4, /device:TPU:0, one launch (start us, length us, event | category | flops | bytes accessed | tf_op | source)
XLA Modules:
  0.0 40.2 jit_solution(8091096804537564976)
XLA Ops:
  0.6 1.2 %turn.1 = (f32[264,128]{1,0:T(8,128)S(1)}, f32[264,128]{1,0:T(8,128)S(1)}, f32[2,8,128]{2,1,0:T(8,128)S(1)}, s32[2,8,128]{2,1,0:T(8,128)S(1)}, f32[3,2,1,128]{3,...) custom-call(f32[128,128]{1,0:T(8,128)} %bitcast.8, ...), custom_call_target="tpu_custom_call" | custom-call | tf_op jit(solution)/shard_map/turn/pallas_call | solution.py:463
  1.8 0.6 %collective-permute-start = (f32[2,8,128]{2,1,0:T(8,128)S(1)}, f32[2,8,128]{2,1,0:T(8,128)S(1)}, u32[]{:S(2)}, u32[]{:S(2)}) collective-permute-start(f32[2,8,128]{2,1,0:T(8,128)S(1)} %get-tuple-element.21), channel_id=1, source_target_pairs={{1,0},{0,1},{3,2},{2,3},{5,4},{4,5},{7,6},{6,7},{9,8},{8,9},{11,10... | collective-permute-start | bytes 24584 | tf_op jit(solution)/shard_map/ppermute | solution.py:29
  2.4 0.9 %observe.1 = (f32[2,128,128]{2,1,0:T(8,128)S(1)}, f32[2,128,128]{2,1,0:T(8,128)S(1)}) custom-call(s32[2,8,128]{2,1,0:T(8,128)S(1)} %get-tuple-element.22.live_ref, s32[2,4,512]{2,1,0:T(4,128)S(1)} %get-tuple-element.23.index_ref, f32[2,4,512]{2,1,0:T(4,128)S(1)} %get-tuple-element.24.weight_ref, f32[2,512]{1,0:T(2,128)S(1)} %get-tuple-element.25.value_ref, ...), custom_call_target="tpu_custom_call" | custom-call | flops 201326592 | bytes 1048576 | tf_op jit(solution)/shard_map/observe/pallas_call | solution.py:495
  3.3 0.0 collective-permute-done.west_ref.east_ref
  3.3 0.1 blocks.1
  3.4 19.6 %all_to_all.10.got_ref = f32[16,40,128]{2,1,0:T(8,128)S(1)} all-to-all(f32[16,40,128]{2,1,0:T(8,128)S(1)} %blocks.1), channel_id=1, replica_groups=mesh['member'=4,'region'=4,'fine'=2] {'member','region'}, dimensions={0} | all-to-all | bytes 655360 | tf_op jit(solution)/shard_map/all_to_all | solution.py:511
  23.0 3.5 %region.1 = f32[16,32,128]{2,1,0:T(8,128)S(1)} custom-call(f32[16,40,128]{2,1,0:T(8,128)S(1)} %all_to_all.10.got_ref, f32[2,128,128]{2,1,0:T(8,128)S(1)} %get-tuple-element.28.info_ref, f32[2,128,128]{2,1,0:T(8,128)S(1)} %get-tuple-element.27.refs_0_.pull_ref), custom_call_target="tpu_custom_call" | custom-call | tf_op jit(solution)/shard_map/region/pallas_call | solution.py:515
  26.5 12.7 %all_to_all.11.got_ref = f32[16,32,128]{2,1,0:T(8,128)S(1)} all-to-all(f32[16,32,128]{2,1,0:T(8,128)S(1)} %region.1), channel_id=1, replica_groups=mesh['member'=4,'region'=4,'fine'=2] {'member','region'}, dimensions={0} | all-to-all | bytes 524288 | tf_op jit(solution)/shard_map/all_to_all | solution.py:538
  39.2 0.9 %home.1 = (f32[128,128]{1,0:T(8,128)}, f32[128,128]{1,0:T(8,128)}, f32[128,128]{1,0:T(8,128)}, f32[3,2,1,128]{3,2,1,0:T(1,128)}) custom-call(f32[16,32,128]{2,1,0:T(8,128)S(1)} %all_to_all.11.got_ref, f32[3,2,1,128]{3,2,1,0:T(1,128)S(1)} %get-tuple-element.29.ctrl_ref), custom_call_target="tpu_custom_call" | custom-call | tf_op jit(solution)/shard_map/home/pallas_call | solution.py:539
Async XLA Ops:
  1.8 1.5 %collective-permute-start = (f32[2,8,128]{2,1,0:T(8,128)S(1)}, f32[2,8,128]{2,1,0:T(8,128)S(1)}, u32[]{:S(2)}, u32[]{:S(2)}) collective-permute-start(f32[2,8,128]{2,1,0:T(8,128)S(1)} %get-tuple-element.21), channel_id=1, source_target_pairs={{1,0},{0,1},{3,2},{2,3},{5,4},{4,5},{7,6},{6,7},{9,8},{8,9},{11,10... | collective-permute-start | bytes 24584 | tf_op jit(solution)/shard_map/ppermute | solution.py:29

commit v5 on v4

--- a/solution.py
+++ b/solution.py
@@ -78,7 +78,7 @@
 
 
 OUT_ROWS = 5 * TILE
-BACK_ROWS = 4 * TILE
+BACK_ROWS = 3 * TILE + 1
 
 
 def turn_kernel(mem, later, *refs):
@@ -304,7 +304,6 @@
         wanted = (lane // width) * cells + s * width + lane % width
         hit = (state == wanted) & (lane < 3 * width)
         row = jnp.sum(jnp.where(hit, increments[q], 0.0), axis=0, keepdims=True)
-        row = jnp.broadcast_to(row, (TILE, LANES))
         for group in range(groups):
             block = group * strips + r
             lanes = slice((group // 2) * LANES, (group // 2 + 1) * LANES)
@@ -315,8 +314,8 @@
                     ana_ref[q, first : first + TILE, lanes],
                     ana_ref[q, first + TILE : first + 2 * TILE, lanes],
                 )
-                send_ref[block, TILE * i : TILE * (i + 1), :] = tile
-            send_ref[block, 3 * TILE : 4 * TILE, :] = row
+                send_ref[BACK_ROWS * block + TILE * i : BACK_ROWS * block + TILE * (i + 1), :] = tile
+            send_ref[BACK_ROWS * (block + 1) - 1 : BACK_ROWS * (block + 1), :] = row
 
 
 def region_kernel(groups, strips, width, got_ref, info_ref, pull_ref, send_ref, x_ref, ana_ref):
@@ -330,15 +329,16 @@
 
 
 def home_kernel(mem, strips, width, got_ref, ctrl_ref, h_ref, u_ref, v_ref, fine_ref):
-    blocks = got_ref.shape[0]
-    tiles = blocks * width // LANES
+    tiles = got_ref.shape[0] // BACK_ROWS * width // LANES
     per_tile = LANES // width
     for i, out_ref in enumerate((h_ref, u_ref, v_ref)):
         for t in range(0, tiles, 2):
             rows = []
             for k in range(per_tile):
-                even = got_ref[t * per_tile + k, TILE * i : TILE * (i + 1), :]
-                odd = got_ref[(t + 1) * per_tile + k, TILE * i : TILE * (i + 1), :]
+                first = BACK_ROWS * (t * per_tile + k) + TILE * i
+                even = got_ref[first : first + TILE, :]
+                first += BACK_ROWS * per_tile
+                odd = got_ref[first : first + TILE, :]
                 rows += [low_pair(even, odd), high_pair(even, odd)]
             turned = jnp.concatenate(rows, axis=0).T
             out_ref[pl.ds(t, mem, stride=tiles), :] = turned[:mem]
@@ -348,8 +348,11 @@
     row = row_of((width, LANES))
     lane = lane_of((width, LANES))
     for t in range(ctrl_ref.shape[3] // LANES):
-        rows = [got_ref[mine + t * per_fine + b, 3 * TILE : 4 * TILE, :] for b in range(per_fine)]
-        columns = [jnp.concatenate([r] * (LANES // TILE), axis=0).T[:, 0:1] for r in rows]
+        rows = [
+            got_ref[pl.ds(BACK_ROWS * (mine + t * per_fine + b) + BACK_ROWS - 1, 1), :]
+            for b in range(per_fine)
+        ]
+        columns = [jnp.broadcast_to(r, (LANES, LANES)).T[:, 0:1] for r in rows]
         for i in range(3):
             total = jnp.zeros((1, LANES), jnp.float32)
             for b in range(per_fine):
@@ -414,6 +417,11 @@
         compiler_params=pltpu.CompilerParams(vmem_limit_bytes=GRANT),
         name=name,
     )
+
+
+def exchanged(blocks, axes, count):
+    dense = blocks.reshape(count, -1, 1, LANES)
+    return lax.all_to_all(dense, axes, split_axis=0, concat_axis=0, tiled=True).reshape(blocks.shape)
 
 
 def f32(*shape):
@@ -509,7 +517,7 @@
         name="blocks",
     )(kept(pair), kept(single), kept(from_west), kept(from_east), *ahead)
     got = kept(lax.all_to_all(out, owners, split_axis=0, concat_axis=0, tiled=True))
-    back_shape = near(count, BACK_ROWS, LANES)
+    back_shape = near(count * BACK_ROWS, LANES)
     layout = (groups, strips, width)
     if small:
         back = call(
@@ -535,7 +543,7 @@
         back = call(
             functools.partial(pack_kernel, *layout), back_shape, [VMEM] * 2, name="pack"
         )(analysis, increment)
-    home = lax.all_to_all(back, owners, split_axis=0, concat_axis=0, tiled=True)
+    home = exchanged(back, owners, count)
     ana_h, ana_u, ana_v, fine_out = call(
         functools.partial(home_kernel, mem, strips, width),
         (f32(*flat), f32(*flat), f32(*flat), f32(*fine_ctrl.shape)),

time: 40.4 us -> 39.1 us (0.968)
  blocking collectives: 32.3 us -> 31.1 us
    all_to_all x1, blocking collectives: 12.7 us -> 11.5 us  [exchanged(): lax.all_to_all(dense, axes, split_axis=0, concat_axis=0, tiled=True)]
where the time goes in v5:
time: 39.1 us; the launch traced here: 38.9 us
  blocking collectives  31.1 us (80%)
  Pallas kernels  6.58 us (17%)
  between operations  0.67 us (2%)
  starting transfers between devices  0.56 us (1%)
    all_to_all x1, blocking collectives, shards(): lax.all_to_all(out, owners, split_axis=0, concat_axis=0, tiled=True)  19.6 us
    all_to_all x1, blocking collectives, exchanged(): lax.all_to_all(dense, axes, split_axis=0, concat_axis=0, tiled=True)  11.5 us
    pallas_call x1, Pallas kernels, shards(): call(functools.partial(region_kernel, *layout), back_shape, [VMEM] * 3, s...  3.52 us
    pallas_call x1, Pallas kernels, shards(): call(functools.partial(turn_kernel, mem, len(later)), (near(columns + TIL...  1.17 us
    pallas_call x1, Pallas kernels, shards(): call(functools.partial(home_kernel, mem, strips, width), (f32(*flat), f32...  0.91 us
    pallas_call x1, Pallas kernels, shards(): call(observe_kernel, (near(REG_DEV, padded, padded), near(REG_DEV, padded...  0.89 us
  transfers between devices with their start and end apart: 1, of which 0 were waited for; matrix products, arithmetic and copies ran while one was open for 0% of the time, Pallas kernels for 2%

profile of v5, /device:TPU:0, one launch (start us, length us, event | category | flops | bytes accessed | tf_op | source)
XLA Modules:
  0.0 38.9 jit_solution(11844649068152164374)
XLA Ops:
  0.6 1.2 %turn.1 = (f32[264,128]{1,0:T(8,128)S(1)}, f32[264,128]{1,0:T(8,128)S(1)}, f32[2,8,128]{2,1,0:T(8,128)S(1)}, s32[2,8,128]{2,1,0:T(8,128)S(1)}, f32[3,2,1,128]{3,...) custom-call(f32[128,128]{1,0:T(8,128)} %bitcast.12, ...), custom_call_target="tpu_custom_call" | custom-call | tf_op jit(solution)/shard_map/turn/pallas_call | solution.py:471
  1.8 0.6 %collective-permute-start = (f32[2,8,128]{2,1,0:T(8,128)S(1)}, f32[2,8,128]{2,1,0:T(8,128)S(1)}, u32[]{:S(2)}, u32[]{:S(2)}) collective-permute-start(f32[2,8,128]{2,1,0:T(8,128)S(1)} %get-tuple-element.21), channel_id=1, source_target_pairs={{1,0},{0,1},{3,2},{2,3},{5,4},{4,5},{7,6},{6,7},{9,8},{8,9},{11,10... | collective-permute-start | bytes 24584 | tf_op jit(solution)/shard_map/ppermute | solution.py:29
  2.4 0.9 %observe.1 = (f32[2,128,128]{2,1,0:T(8,128)S(1)}, f32[2,128,128]{2,1,0:T(8,128)S(1)}) custom-call(s32[2,8,128]{2,1,0:T(8,128)S(1)} %get-tuple-element.22.live_ref, s32[2,4,512]{2,1,0:T(4,128)S(1)} %get-tuple-element.23.index_ref, f32[2,4,512]{2,1,0:T(4,128)S(1)} %get-tuple-element.24.weight_ref, f32[2,512]{1,0:T(2,128)S(1)} %get-tuple-element.25.value_ref, ...), custom_call_target="tpu_custom_call" | custom-call | flops 201326592 | bytes 1048576 | tf_op jit(solution)/shard_map/observe/pallas_call | solution.py:503
  3.3 0.0 collective-permute-done.west_ref.east_ref
  3.3 0.1 blocks.1
  3.4 19.6 %all_to_all.10.got_ref = f32[16,40,128]{2,1,0:T(8,128)S(1)} all-to-all(f32[16,40,128]{2,1,0:T(8,128)S(1)} %blocks.1), channel_id=1, replica_groups=mesh['member'=4,'region'=4,'fine'=2] {'member','region'}, dimensions={0} | all-to-all | bytes 655360 | tf_op jit(solution)/shard_map/all_to_all | solution.py:519
  23.0 3.5 %region.1 = f32[400,128]{1,0:T(8,128)S(1)} custom-call(f32[16,40,128]{2,1,0:T(8,128)S(1)} %all_to_all.10.got_ref, f32[2,128,128]{2,1,0:T(8,128)S(1)} %get-tuple-element.28.info_ref, f32[2,128,128]{2,1,0:T(8,128)S(1)} %get-tuple-element.27.refs_0_.pull_ref), custom_call_target="tpu_custom_call" | custom-call | tf_op jit(solution)/shard_map/region/pallas_call | solution.py:523
  26.5 11.5 %all_to_all.11 = f32[16,25,1,128]{3,2,1,0:T(1,128)S(1)} all-to-all(f32[16,25,1,128]{3,2,1,0:T(1,128)S(1)} %bitcast.11), channel_id=1, replica_groups=mesh['member'=4,'region'=4,'fine'=2] {'member','region'}, dimensions={0} | all-to-all | bytes 409600 | tf_op jit(solution)/shard_map/all_to_all | solution.py:424
  38.0 0.9 %home.1 = (f32[128,128]{1,0:T(8,128)}, f32[128,128]{1,0:T(8,128)}, f32[128,128]{1,0:T(8,128)}, f32[3,2,1,128]{3,2,1,0:T(1,128)}) custom-call(f32[400,128]{1,0:T(8,128)S(1)} %bitcast.10, f32[3,2,1,128]{3,2,1,0:T(1,128)S(1)} %get-tuple-element.29.ctrl_ref), custom_call_target="tpu_custom_call" | custom-call | tf_op jit(solution)/shard_map/home/pallas_call | solution.py:547
Async XLA Ops:
  1.8 1.5 %collective-permute-start = (f32[2,8,128]{2,1,0:T(8,128)S(1)}, f32[2,8,128]{2,1,0:T(8,128)S(1)}, u32[]{:S(2)}, u32[]{:S(2)}) collective-permute-start(f32[2,8,128]{2,1,0:T(8,128)S(1)} %get-tuple-element.21), channel_id=1, source_target_pairs={{1,0},{0,1},{3,2},{2,3},{5,4},{4,5},{7,6},{6,7},{9,8},{8,9},{11,10... | collective-permute-start | bytes 24584 | tf_op jit(solution)/shard_map/ppermute | solution.py:29
